TPU v7x, 256 devices: a whole 4x4x8 slice. The times are simulated.
256 devices in a mesh: sta: 64 (over z, y, core), win: 4 (over x).
Axes of the slice: x: 4, y: 4, z: 8, core: 2. Of those that a mesh axis runs over, the one named last changes fastest.
Arguments:
- spectra: bfloat16 [64, 448, 4096], P('win', 'sta'), may hold values from -6 to 6
- pair_bins: int32 [448, 3, 7], P('sta'), may hold values from 0 to 127
- owner_count: int32 [64], replicated, may hold values from 1 to 4, 128 in all
- bin_order: int32 [128], replicated, may hold values from 0 to 127, each once
Outputs:
- owned_stacks: float32 [256, 4096], P('sta', 'win')
Inputs may be any that keep to these rules, and one draw needn't show every extreme that they name: Owner o holds owner_count[o] bins; the counts sum to 128 and the largest is exactly 4. `bin_order`: every bin appears exactly once.
All inputs are finite; a program needn't handle non-finite values.
Results may differ from a plain program's by a relative error of at most 0.0011.
Values may be sent and summed in bfloat16 or wider, within the bound.
No kernel may reach another device: no remote copies, remote signals or barrier semaphores. Data moves between devices by JAX's collectives and lax.ppermute only.
A program may use at most 128 MiB of HBM per device.

v0:
```python
import jax
import jax.numpy as jnp
from jax import lax
from jax.experimental import pallas as pl
from jax.experimental.pallas import tpu as pltpu
from jax.sharding import Mesh, PartitionSpec as P

PLANE = 8
STA = 7
WIN = 16
NG = 4
ROUNDS = 3
CAP = 4
ROWS = STA * WIN
MSG = ROWS + 8
LANES = 128
CHUNK = 32
KI = 256
F32 = jnp.float32
BF16 = jnp.bfloat16


def lane_iota(shape):
    return lax.broadcasted_iota(jnp.int32, shape, len(shape) - 1)


def chunk_transpose(tiles):
    lane = lane_iota(tiles[0].shape)
    low = lane < 64
    even = (lane % 64) < CHUNK
    axis = tiles[0].ndim - 1

    def half(a, b):
        return jnp.where(low, a, pltpu.roll(b, 64, axis)), jnp.where(low, pltpu.roll(a, 64, axis), b)

    def quarter(a, b):
        return jnp.where(even, a, pltpu.roll(b, CHUNK, axis)), jnp.where(even, pltpu.roll(a, LANES - CHUNK, axis), b)

    u0, u2 = half(tiles[0], tiles[2])
    u1, u3 = half(tiles[1], tiles[3])
    v0, v1 = quarter(u0, u1)
    v2, v3 = quarter(u2, u3)
    return v0, v1, v2, v3


def pack_kernel(x_ref, bins_ref, out_ref):
    lane8 = lax.broadcasted_iota(jnp.int32, (STA, LANES), 1)
    row8 = lax.broadcasted_iota(jnp.int32, (STA, LANES), 0)
    labels = jnp.zeros((STA, LANES), F32)
    for r in range(ROUNDS):
        place = jnp.where(lane8 == row8 + 8 * r, 1.0, 0.0).astype(F32)
        labels = labels + jnp.dot(bins_ref[r].astype(F32), place, preferred_element_type=F32)
    labels = jnp.concatenate([labels, jnp.zeros((1, LANES), F32)], axis=0).astype(BF16)

    def step(q, carry):
        col = pl.multiple_of(q * LANES, LANES)
        for s in range(STA):
            tiles = [x_ref[s, :, pl.ds(n * 1024 + col, LANES)].astype(F32) for n in range(4)]
            for m, tile in enumerate(chunk_transpose(tiles)):
                out_ref[4 * q + m, s * WIN:(s + 1) * WIN, :] = tile.astype(BF16)
        for m in range(4):
            out_ref[4 * q + m, ROWS:MSG, :] = labels
        return carry

    lax.fori_loop(0, 8, step, 0)


def slot_bins(count_ref, order_ref):
    row = lax.broadcasted_iota(jnp.int32, (64, 64), 0)
    lane = lax.broadcasted_iota(jnp.int32, (64, 64), 1)
    counts = jnp.broadcast_to(count_ref[...].astype(F32), (64, 64))
    start = jnp.sum(jnp.where(lane < row, counts, 0.0), axis=1, keepdims=True)
    count = jnp.sum(jnp.where(lane == row, counts, 0.0), axis=1, keepdims=True)
    lane = lax.broadcasted_iota(jnp.int32, (64, LANES), 1).astype(F32)
    order = jnp.broadcast_to(order_ref[...].astype(F32), (64, LANES))
    out = []
    for k in range(CAP):
        chosen = jnp.sum(jnp.where(lane == start + float(k), order, 0.0), axis=1, keepdims=True)
        out.append(jnp.where(count > float(k), chosen, -1.0))
    return out


def cross_kernel(own_ref, halo_ref, count_ref, order_ref, out_ref, c_ref, cs_ref, f_ref, x_ref, hot_ref):
    lane = lane_iota((8, LANES))
    low = lane < 64
    zero = jnp.zeros((8, LANES), F32)

    spread = jnp.where(lax.broadcasted_iota(jnp.int32, (LANES, KI), 1) // 8
                       == lax.broadcasted_iota(jnp.int32, (LANES, KI), 0), 1.0, 0.0)
    qmod = lax.broadcasted_iota(jnp.int32, (8, KI), 1) % 8
    labels = jnp.zeros((8, KI), F32)
    for b in range(PLANE):
        wide = jnp.dot(own_ref[b * NG, ROWS:MSG, :].astype(F32), spread, preferred_element_type=F32)
        labels = labels + jnp.where(qmod == b, wide, 0.0)
    bins = [jnp.broadcast_to(v, (64, KI)) for v in slot_bins(count_ref, order_ref)]
    for i in range(STA):
        row = jnp.broadcast_to(labels[i:i + 1, :], (64, KI))
        for k in range(CAP):
            hot_ref[k * 64:(k + 1) * 64, i * KI:(i + 1) * KI] = jnp.where(bins[k] == row, 1.0, 0.0).astype(BF16)

    for i in range(STA):
        for r in range(ROUNDS):
            f_ref[i, (r * 8 + 7) * 8:(r * 8 + 8) * 8, :] = zero
        for n in range(8):
            f_ref[i, (24 + n) * 8:(25 + n) * 8, :] = zero

    def per_shard(g, carry):
        sign = jnp.where(lane_iota((ROWS, LANES)) < 64, -1.0, 1.0).astype(F32)
        for bb in range(PLANE + 2):
            if bb < 2:
                piece = halo_ref[bb * NG + g, 0:ROWS, :]
            else:
                piece = own_ref[(bb - 2) * NG + g, 0:ROWS, :]
            piece = piece.astype(F32)
            turned = pltpu.roll(piece, 64, 1) * sign
            for s in range(STA):
                c_ref[s, bb * WIN:(bb + 1) * WIN, :] = piece[s * WIN:(s + 1) * WIN, :]
                cs_ref[s, bb * WIN:(bb + 1) * WIN, :] = turned[s * WIN:(s + 1) * WIN, :]

        def put(i, r, j, value):
            f_ref[i, (r * 8 + j) * 8:(r * 8 + j + 1) * 8, :] = value

        def joined(p, q):
            return jnp.where(low, p, q) + pltpu.roll(jnp.where(low, q, p), 64, 1)

        def group(pairs, r):
            own = sorted({i for i, _ in pairs})
            other = sorted({j for _, j in pairs})
            acc_p, acc_q = {}, {}
            for w in range(WIN):
                a = {i: c_ref[i, pl.ds(2 * WIN + w, 8, stride=WIN), :] for i in own}
                for j in other:
                    c = c_ref[j, pl.ds((2 - r) * WIN + w, 8, stride=WIN), :]
                    d = cs_ref[j, pl.ds((2 - r) * WIN + w, 8, stride=WIN), :]
                    for i in own:
                        if (i, j) not in pairs:
                            continue
                        p = a[i] * c
                        acc_p[i, j] = p if w == 0 else acc_p[i, j] + p
                        if r == 0 and i == j:
                            continue
                        q = a[i] * d
                        acc_q[i, j] = q if w == 0 else acc_q[i, j] + q
            for i, j in pairs:
                value = joined(acc_p[i, j], acc_q.get((i, j), zero))
                put(i, r, j, value)
                if r == 0 and i != j:
                    put(j, r, i, jnp.where(low, value, -value))

        for own in ((0, 1), (2, 3), (4, 5, 6)):
            group([(i, j) for i in own for j in range(i, STA)], 0)
        for r in (1, 2):
            for own in ((0, 1), (2, 3), (4, 5), (6,)):
                group([(i, j) for i in own for j in range(STA)], r)
        for i in range(STA):
            x_ref[i * KI:(i + 1) * KI, pl.ds(pl.multiple_of(g * LANES, LANES), LANES)] = f_ref[i].astype(BF16)
        return carry

    lax.fori_loop(0, NG, per_shard, 0)
    total = jnp.dot(hot_ref[...], x_ref[...], preferred_element_type=F32)
    total = (total[:, 0:128] + total[:, 128:256]) + (total[:, 256:384] + total[:, 384:512])
    for w, tile in enumerate(chunk_transpose([total[k * 64:(k + 1) * 64, :] for k in range(CAP)])):
        out_ref[pl.ds(w, 64, stride=4), :] = tile


def finish_kernel(in_ref, out_ref, s_ref):
    total = in_ref[0]
    for z in range(1, 8):
        total = total + in_ref[z]
    s_ref[...] = total * (1.0 / 64.0)
    tiles = chunk_transpose([s_ref[pl.ds(m, 8, stride=4), :] for m in range(4)])
    for k in range(CAP):
        for t in range(8):
            out_ref[k:k + 1, t * LANES:(t + 1) * LANES] = tiles[k][t:t + 1, :]


def on_device(spectra, pair_bins, owner_count, bin_order):
    vmem = pl.BlockSpec(memory_space=pltpu.VMEM)
    packed = pl.pallas_call(
        pack_kernel,
        out_shape=jax.ShapeDtypeStruct((32, MSG, LANES), BF16),
        in_specs=[vmem, vmem],
        out_specs=vmem,
        name="pack",
    )(jnp.transpose(spectra, (1, 0, 2)), jnp.transpose(pair_bins, (1, 0, 2)))
    own = lax.all_to_all(packed, ("y", "c", "win"), 0, 0)
    count = lax.axis_size("z")
    halo = lax.ppermute(own[24:32], "z", [(i, (i + 1) % count) for i in range(count)])
    send = pl.pallas_call(
        cross_kernel,
        out_shape=jax.ShapeDtypeStruct((256, LANES), F32),
        in_specs=[vmem] * 4,
        out_specs=vmem,
        scratch_shapes=[
            pltpu.VMEM((STA, (PLANE + 2) * WIN, LANES), F32),
            pltpu.VMEM((STA, (PLANE + 2) * WIN, LANES), F32),
            pltpu.VMEM((STA, KI, LANES), F32),
            pltpu.VMEM((STA * KI, NG * LANES), BF16),
            pltpu.VMEM((256, STA * KI), BF16),
        ],
        name="cross",
    )(own, halo, owner_count.reshape(1, -1), bin_order.reshape(1, -1))
    got = lax.all_to_all(send.reshape(256, 1, LANES), ("z", "y", "c", "win"), 0, 0)
    return pl.pallas_call(
        finish_kernel,
        out_shape=jax.ShapeDtypeStruct((CAP, 1024), F32),
        in_specs=[vmem],
        out_specs=vmem,
        scratch_shapes=[pltpu.VMEM((32, LANES), F32)],
        name="finish",
    )(got.reshape(8, 32, LANES))


def solution(mesh):
    fine = Mesh(mesh.devices.reshape(8, 4, 2, 4), ("z", "y", "c", "win"))
    sta = ("z", "y", "c")
    return jax.shard_map(
        on_device,
        mesh=fine,
        in_specs=(P("win", sta, None), P(sta, None, None), P(), P()),
        out_specs=P(sta, "win"),
        check_vma=False,
    )
```

profile of v0, /device:TPU:1, one launch (start us, length us, event | category | flops | bytes accessed | tf_op | source)
XLA Modules:
  0.0 81.0 jit_solution(11522872107737354096)
XLA Ops:
  0.0 3.8 %pack.1 = bf16[32,120,128]{2,1,0:T(8,128)(2,1)} custom-call(bf16[7,16,4096]{2,1,0:T(8,128)(2,1)} %bitcast.8, s32[3,7,7]{2,1,0:T(8,128)} %bitcast.11), custom_call_target="tpu_custom_call" | custom-call | tf_op jit(solution)/shard_map/pack/pallas_call | solution.py:179
  3.8 24.0 %all_to_all.10.own_ref = bf16[32,120,128]{2,1,0:T(8,128)(2,1)S(1)} all-to-all(bf16[32,120,128]{2,1,0:T(8,128)(2,1)} %pack.1), channel_id=1, replica_groups=mesh['z'=8,'y'=4,'c'=2,'win'=4] {'y','c','win'}, dimensions={0} | all-to-all | bytes 1966080 | tf_op jit(solution)/shard_map/all_to_all | solution.py:186
  27.8 0.0 copy-start
  27.8 1.7 %collective-permute-start = (bf16[8,120,128]{2,1,0:T(8,128)(2,1)S(1)}, bf16[8,120,128]{2,1,0:T(8,128)(2,1)S(1)}, u32[]{:S(2)}, u32[]{:S(2)}) collective-permute-start(bf16[8,120,128]{2,1,0:T(8,128)(2,1)S(1)} %slice.4), channel_id=1, source_target_pairs={{0,32},{32,64},{64,96},{96,128},{128,160},{160,192},{192,224},{224... | collective-permute-start | bytes 737288 | tf_op jit(solution)/shard_map/ppermute | solution.py:188
  29.5 9.1 %collective-permute-done.halo_ref = bf16[8,120,128]{2,1,0:T(8,128)(2,1)S(1)} collective-permute-done((bf16[8,120,128]{2,1,0:T(8,128)(2,1)S(1)}, bf16[8,120,128]{2,1,0:T(8,128)(2,1)S(1)}, u32[]{:S(2)}, u32[]{:S(2)}) %collective-permute-start) | collective-permute-done | bytes 245792 | tf_op jit(solution)/shard_map/ppermute | solution.py:188
  38.6 0.0 copy-start.1
  38.6 0.0 copy-done
  38.6 0.7 copy-done.1
  39.3 17.1 %cross.1 = f32[256,128]{1,0:T(8,128)} custom-call(bf16[32,120,128]{2,1,0:T(8,128)(2,1)} %copy-done, bf16[8,120,128]{2,1,0:T(8,128)(2,1)} %copy-done.1, s32[1,64]{1,0:T(1,128)} %bitcast.12, s32[1,128]{1,0:T(1,128)} %bitcast.13), custom_call_target="tpu_custom_call" | custom-call | tf_op jit(solution)/shard_map/cross/pallas_call | solution.py:189
  56.5 22.9 %all_to_all.11 = f32[256,1,128]{2,1,0:T(1,128)} all-to-all(f32[256,1,128]{2,1,0:T(1,128)} %bitcast.9), channel_id=1, replica_groups=mesh['z'=8,'y'=4,'c'=2,'win'=4] {'z','y','c','win'}, dimensions={0} | all-to-all | bytes 262144 | tf_op jit(solution)/shard_map/all_to_all | solution.py:203
  79.4 1.7 %finish.1 = f32[4,1024]{1,0:T(4,128)} custom-call(f32[8,32,128]{2,1,0:T(8,128)} %bitcast.10), custom_call_target="tpu_custom_call" | custom-call | tf_op jit(solution)/shard_map/finish/pallas_call | solution.py:204
  (1 shorter events, 0.0 us)
Async XLA Ops:
  27.8 10.8 %copy-start = (bf16[32,120,128]{2,1,0:T(8,128)(2,1)}, bf16[32,120,128]{2,1,0:T(8,128)(2,1)S(1)}, u32[]{:S(2)}) copy-start(bf16[32,120,128]{2,1,0:T(8,128)(2,1)S(1)} %all_to_all.10.own_ref) | copy-start | bytes 2949124
  27.8 10.8 %collective-permute-start = (bf16[8,120,128]{2,1,0:T(8,128)(2,1)S(1)}, bf16[8,120,128]{2,1,0:T(8,128)(2,1)S(1)}, u32[]{:S(2)}, u32[]{:S(2)}) collective-permute-start(bf16[8,120,128]{2,1,0:T(8,128)(2,1)S(1)} %slice.4), channel_id=1, source_target_pairs={{0,32},{32,64},{64,96},{96,128},{128,160},{160,192},{192,224},{224... | collective-permute-start | bytes 737288 | tf_op jit(solution)/shard_map/ppermute | solution.py:188
  38.6 0.7 copy-start.1
where the time goes:
time: 81.3 us; the launch traced here: 81 us
  blocking collectives  46.9 us (58%)
  Pallas kernels  22.6 us (28%)
  waiting for transfers between devices  9.1 us (11%)
  starting transfers between devices  1.71 us (2%)
    all_to_all x1, blocking collectives, on_device(): own = lax.all_to_all(packed, ('y', 'c', 'win'), 0, 0)  24 us
    all_to_all x1, blocking collectives, on_device(): lax.all_to_all(send.reshape(256, 1, LANES), ('z', 'y', 'c', 'win'), 0, 0)  22.9 us
    pallas_call x1, Pallas kernels, on_device(): pl.pallas_call(cross_kernel, out_shape=jax.ShapeDtypeStruct((256, LANES),...  17.1 us
    ppermute x1, waiting for transfers between devices, on_device(): lax.ppermute(own[24:32], 'z', [(i, (i + 1) % count) for i in range(count)])  9.1 us
    pallas_call x1, Pallas kernels, on_device(): pl.pallas_call(pack_kernel, out_shape=jax.ShapeDtypeStruct((32, MSG, LANE...  3.76 us
    ppermute x1, starting transfers between devices, on_device(): lax.ppermute(own[24:32], 'z', [(i, (i + 1) % count) for i in range(count)])  1.71 us
    pallas_call x1, Pallas kernels, on_device(): pl.pallas_call(finish_kernel, out_shape=jax.ShapeDtypeStruct((CAP, 1024),...  1.67 us
  transfers between devices with their start and end apart: 1, of which 1 were waited for; matrix products, arithmetic and copies ran while one was open for 0% of the time, Pallas kernels for 0%

commit v1 on v0

--- a/solution.py
+++ b/solution.py
@@ -13,6 +13,7 @@
 CAP = 4
 ROWS = STA * WIN
 MSG = ROWS + 8
+PITCH = WIN + 1
 LANES = 128
 CHUNK = 32
 KI = 256
@@ -55,9 +56,9 @@
     def step(q, carry):
         col = pl.multiple_of(q * LANES, LANES)
         for s in range(STA):
-            tiles = [x_ref[s, :, pl.ds(n * 1024 + col, LANES)].astype(F32) for n in range(4)]
+            tiles = [x_ref[s, :, pl.ds(n * 1024 + col, LANES)] for n in range(4)]
             for m, tile in enumerate(chunk_transpose(tiles)):
-                out_ref[4 * q + m, s * WIN:(s + 1) * WIN, :] = tile.astype(BF16)
+                out_ref[4 * q + m, s * WIN:(s + 1) * WIN, :] = tile
         for m in range(4):
             out_ref[4 * q + m, ROWS:MSG, :] = labels
         return carry
@@ -80,7 +81,7 @@
     return out
 
 
-def cross_kernel(own_ref, halo_ref, count_ref, order_ref, out_ref, c_ref, cs_ref, f_ref, x_ref, hot_ref):
+def cross_kernel(own_ref, halo_ref, count_ref, order_ref, out_ref, c_ref, t_ref, f_ref, x_ref, hot_ref):
     lane = lane_iota((8, LANES))
     low = lane < 64
     zero = jnp.zeros((8, LANES), F32)
@@ -99,61 +100,59 @@
             hot_ref[k * 64:(k + 1) * 64, i * KI:(i + 1) * KI] = jnp.where(bins[k] == row, 1.0, 0.0).astype(BF16)
 
     for i in range(STA):
-        for r in range(ROUNDS):
-            f_ref[i, (r * 8 + 7) * 8:(r * 8 + 8) * 8, :] = zero
-        for n in range(8):
-            f_ref[i, (24 + n) * 8:(25 + n) * 8, :] = zero
+        f_ref[i, STA * 8:(STA + 1) * 8, :] = zero
+        x_ref[i * KI + ROUNDS * 64:(i + 1) * KI, :] = jnp.zeros((64, NG * LANES), BF16)
 
     def per_shard(g, carry):
-        sign = jnp.where(lane_iota((ROWS, LANES)) < 64, -1.0, 1.0).astype(F32)
+        sign = jnp.where(lane_iota((ROWS, LANES)) < 64, 1.0, -1.0).astype(F32)
         for bb in range(PLANE + 2):
             if bb < 2:
-                piece = halo_ref[bb * NG + g, 0:ROWS, :]
+                piece = halo_ref[bb * NG + g, 0:ROWS, :].astype(F32)
             else:
-                piece = own_ref[(bb - 2) * NG + g, 0:ROWS, :]
-            piece = piece.astype(F32)
-            turned = pltpu.roll(piece, 64, 1) * sign
+                piece = own_ref[(bb - 2) * NG + g, 0:ROWS, :].astype(F32)
+                turned = pltpu.roll(piece, 64, 1) * sign
             for s in range(STA):
-                c_ref[s, bb * WIN:(bb + 1) * WIN, :] = piece[s * WIN:(s + 1) * WIN, :]
-                cs_ref[s, bb * WIN:(bb + 1) * WIN, :] = turned[s * WIN:(s + 1) * WIN, :]
-
-        def put(i, r, j, value):
-            f_ref[i, (r * 8 + j) * 8:(r * 8 + j + 1) * 8, :] = value
+                rows = slice(s * WIN, (s + 1) * WIN)
+                c_ref[s, bb * PITCH:bb * PITCH + WIN, :] = piece[rows]
+                if bb >= 2:
+                    t_ref[s, (bb - 2) * PITCH:(bb - 2) * PITCH + WIN, :] = turned[rows]
+
+        lanes = pl.ds(pl.multiple_of(g * LANES, LANES), LANES)
 
         def joined(p, q):
             return jnp.where(low, p, q) + pltpu.roll(jnp.where(low, q, p), 64, 1)
 
-        def group(pairs, r):
-            own = sorted({i for i, _ in pairs})
-            other = sorted({j for _, j in pairs})
-            acc_p, acc_q = {}, {}
+        def row_of(i, r, others):
+            p, q = {}, {}
             for w in range(WIN):
-                a = {i: c_ref[i, pl.ds(2 * WIN + w, 8, stride=WIN), :] for i in own}
-                for j in other:
-                    c = c_ref[j, pl.ds((2 - r) * WIN + w, 8, stride=WIN), :]
-                    d = cs_ref[j, pl.ds((2 - r) * WIN + w, 8, stride=WIN), :]
-                    for i in own:
-                        if (i, j) not in pairs:
-                            continue
-                        p = a[i] * c
-                        acc_p[i, j] = p if w == 0 else acc_p[i, j] + p
-                        if r == 0 and i == j:
-                            continue
-                        q = a[i] * d
-                        acc_q[i, j] = q if w == 0 else acc_q[i, j] + q
-            for i, j in pairs:
-                value = joined(acc_p[i, j], acc_q.get((i, j), zero))
-                put(i, r, j, value)
-                if r == 0 and i != j:
-                    put(j, r, i, jnp.where(low, value, -value))
-
-        for own in ((0, 1), (2, 3), (4, 5, 6)):
-            group([(i, j) for i in own for j in range(i, STA)], 0)
-        for r in (1, 2):
-            for own in ((0, 1), (2, 3), (4, 5), (6,)):
-                group([(i, j) for i in own for j in range(STA)], r)
+                a = c_ref[i, pl.ds(2 * PITCH + w, 8, stride=PITCH), :]
+                t = t_ref[i, pl.ds(w, 8, stride=PITCH), :]
+                for j in others:
+                    if r == 0 and j == i:
+                        v = a * a
+                        p[j] = v if w == 0 else p[j] + v
+                        continue
+                    c = c_ref[j, pl.ds((2 - r) * PITCH + w, 8, stride=PITCH), :]
+                    v = a * c
+                    p[j] = v if w == 0 else p[j] + v
+                    v = t * c
+                    q[j] = v if w == 0 else q[j] + v
+            return {j: joined(p[j], q.get(j, zero)) for j in others}
+
         for i in range(STA):
-            x_ref[i * KI:(i + 1) * KI, pl.ds(pl.multiple_of(g * LANES, LANES), LANES)] = f_ref[i].astype(BF16)
+            for j, value in row_of(i, 0, list(range(i, STA))).items():
+                f_ref[i, j * 8:(j + 1) * 8, :] = value
+                if j != i:
+                    f_ref[j, i * 8:(i + 1) * 8, :] = jnp.where(low, value, -value)
+            for r in (1, 2):
+                values = row_of(i, r, list(range(STA)))
+                values[STA] = zero
+                for j in range(0, 8, 2):
+                    pair = jnp.concatenate([values[j], values[j + 1]], axis=0).astype(BF16)
+                    base = i * KI + (r * 8 + j) * 8
+                    x_ref[base:base + 16, lanes] = pair
+        for i in range(STA):
+            x_ref[i * KI:i * KI + 64, lanes] = f_ref[i].astype(BF16)
         return carry
 
     lax.fori_loop(0, NG, per_shard, 0)
@@ -192,9 +191,9 @@
         in_specs=[vmem] * 4,
         out_specs=vmem,
         scratch_shapes=[
-            pltpu.VMEM((STA, (PLANE + 2) * WIN, LANES), F32),
-            pltpu.VMEM((STA, (PLANE + 2) * WIN, LANES), F32),
-            pltpu.VMEM((STA, KI, LANES), F32),
+            pltpu.VMEM((STA, 176, LANES), F32),
+            pltpu.VMEM((STA, 144, LANES), F32),
+            pltpu.VMEM((STA, 64, LANES), F32),
             pltpu.VMEM((STA * KI, NG * LANES), BF16),
             pltpu.VMEM((256, STA * KI), BF16),
         ],

time: 81.3 us -> 73.5 us (0.904)
  Pallas kernels: 22.6 us -> 14.7 us
    pallas_call x1, Pallas kernels: 17.1 us -> 9.3 us  [on_device(): pl.pallas_call(cross_kernel, out_shape=jax.ShapeDtypeStruct((256, LANES),...]
where the time goes in v1:
time: 73.5 us; the launch traced here: 73.2 us
  blocking collectives  46.9 us (64%)
  Pallas kernels  14.7 us (20%)
  waiting for transfers between devices  9.1 us (12%)
  starting transfers between devices  1.71 us (2%)
    all_to_all x1, blocking collectives, on_device(): own = lax.all_to_all(packed, ('y', 'c', 'win'), 0, 0)  24 us
    all_to_all x1, blocking collectives, on_device(): lax.all_to_all(send.reshape(256, 1, LANES), ('z', 'y', 'c', 'win'), 0, 0)  22.9 us
    pallas_call x1, Pallas kernels, on_device(): pl.pallas_call(cross_kernel, out_shape=jax.ShapeDtypeStruct((256, LANES),...  9.3 us
    ppermute x1, waiting for transfers between devices, on_device(): lax.ppermute(own[24:32], 'z', [(i, (i + 1) % count) for i in range(count)])  9.1 us
    pallas_call x1, Pallas kernels, on_device(): pl.pallas_call(pack_kernel, out_shape=jax.ShapeDtypeStruct((32, MSG, LANE...  3.76 us
    ppermute x1, starting transfers between devices, on_device(): lax.ppermute(own[24:32], 'z', [(i, (i + 1) % count) for i in range(count)])  1.71 us
    pallas_call x1, Pallas kernels, on_device(): pl.pallas_call(finish_kernel, out_shape=jax.ShapeDtypeStruct((CAP, 1024),...  1.67 us
  transfers between devices with their start and end apart: 1, of which 1 were waited for; matrix products, arithmetic and copies ran while one was open for 0% of the time, Pallas kernels for 0%

profile of v1, /device:TPU:1, one launch (start us, length us, event | category | flops | bytes accessed | tf_op | source)
XLA Modules:
  0.0 73.2 jit_solution(9220391327065201063)
XLA Ops:
  0.0 3.8 %pack.1 = bf16[32,120,128]{2,1,0:T(8,128)(2,1)} custom-call(bf16[7,16,4096]{2,1,0:T(8,128)(2,1)} %bitcast.8, s32[3,7,7]{2,1,0:T(8,128)} %bitcast.11), custom_call_target="tpu_custom_call" | custom-call | tf_op jit(solution)/shard_map/pack/pallas_call | solution.py:178
  3.8 24.0 %all_to_all.10.own_ref = bf16[32,120,128]{2,1,0:T(8,128)(2,1)S(1)} all-to-all(bf16[32,120,128]{2,1,0:T(8,128)(2,1)} %pack.1), channel_id=1, replica_groups=mesh['z'=8,'y'=4,'c'=2,'win'=4] {'y','c','win'}, dimensions={0} | all-to-all | bytes 1966080 | tf_op jit(solution)/shard_map/all_to_all | solution.py:185
  27.8 0.0 copy-start
  27.8 1.7 %collective-permute-start = (bf16[8,120,128]{2,1,0:T(8,128)(2,1)S(1)}, bf16[8,120,128]{2,1,0:T(8,128)(2,1)S(1)}, u32[]{:S(2)}, u32[]{:S(2)}) collective-permute-start(bf16[8,120,128]{2,1,0:T(8,128)(2,1)S(1)} %slice.4), channel_id=1, source_target_pairs={{0,32},{32,64},{64,96},{96,128},{128,160},{160,192},{192,224},{224... | collective-permute-start | bytes 737288 | tf_op jit(solution)/shard_map/ppermute | solution.py:187
  29.5 9.1 %collective-permute-done.halo_ref = bf16[8,120,128]{2,1,0:T(8,128)(2,1)S(1)} collective-permute-done((bf16[8,120,128]{2,1,0:T(8,128)(2,1)S(1)}, bf16[8,120,128]{2,1,0:T(8,128)(2,1)S(1)}, u32[]{:S(2)}, u32[]{:S(2)}) %collective-permute-start) | collective-permute-done | bytes 245792 | tf_op jit(solution)/shard_map/ppermute | solution.py:187
  38.6 0.0 copy-start.1
  38.6 0.0 copy-done
  38.6 0.7 copy-done.1
  39.3 9.3 %cross.1 = f32[256,128]{1,0:T(8,128)} custom-call(bf16[32,120,128]{2,1,0:T(8,128)(2,1)} %copy-done, bf16[8,120,128]{2,1,0:T(8,128)(2,1)} %copy-done.1, s32[1,64]{1,0:T(1,128)} %bitcast.12, s32[1,128]{1,0:T(1,128)} %bitcast.13), custom_call_target="tpu_custom_call" | custom-call | tf_op jit(solution)/shard_map/cross/pallas_call | solution.py:188
  48.6 22.9 %all_to_all.11 = f32[256,1,128]{2,1,0:T(1,128)} all-to-all(f32[256,1,128]{2,1,0:T(1,128)} %bitcast.9), channel_id=1, replica_groups=mesh['z'=8,'y'=4,'c'=2,'win'=4] {'z','y','c','win'}, dimensions={0} | all-to-all | bytes 262144 | tf_op jit(solution)/shard_map/all_to_all | solution.py:202
  71.5 1.7 %finish.1 = f32[4,1024]{1,0:T(4,128)} custom-call(f32[8,32,128]{2,1,0:T(8,128)} %bitcast.10), custom_call_target="tpu_custom_call" | custom-call | tf_op jit(solution)/shard_map/finish/pallas_call | solution.py:203
  (1 shorter events, 0.0 us)
Async XLA Ops:
  27.8 10.8 %copy-start = (bf16[32,120,128]{2,1,0:T(8,128)(2,1)}, bf16[32,120,128]{2,1,0:T(8,128)(2,1)S(1)}, u32[]{:S(2)}) copy-start(bf16[32,120,128]{2,1,0:T(8,128)(2,1)S(1)} %all_to_all.10.own_ref) | copy-start | bytes 2949124
  27.8 10.8 %collective-permute-start = (bf16[8,120,128]{2,1,0:T(8,128)(2,1)S(1)}, bf16[8,120,128]{2,1,0:T(8,128)(2,1)S(1)}, u32[]{:S(2)}, u32[]{:S(2)}) collective-permute-start(bf16[8,120,128]{2,1,0:T(8,128)(2,1)S(1)} %slice.4), channel_id=1, source_target_pairs={{0,32},{32,64},{64,96},{96,128},{128,160},{160,192},{192,224},{224... | collective-permute-start | bytes 737288 | tf_op jit(solution)/shard_map/ppermute | solution.py:187
  38.6 0.7 copy-start.1

commit v2 on v1

--- a/solution.py
+++ b/solution.py
@@ -44,7 +44,12 @@
     return v0, v1, v2, v3
 
 
-def pack_kernel(x_ref, bins_ref, out_ref):
+def pack_kernel(x_hbm, bins_ref, out_ref, x_ref, sems):
+    def station(s):
+        return pltpu.make_async_copy(x_hbm.at[s], x_ref.at[s], sems.at[s])
+
+    for s in range(STA):
+        station(s).start()
     lane8 = lax.broadcasted_iota(jnp.int32, (STA, LANES), 1)
     row8 = lax.broadcasted_iota(jnp.int32, (STA, LANES), 0)
     labels = jnp.zeros((STA, LANES), F32)
@@ -53,17 +58,19 @@
         labels = labels + jnp.dot(bins_ref[r].astype(F32), place, preferred_element_type=F32)
     labels = jnp.concatenate([labels, jnp.zeros((1, LANES), F32)], axis=0).astype(BF16)
 
-    def step(q, carry):
-        col = pl.multiple_of(q * LANES, LANES)
-        for s in range(STA):
-            tiles = [x_ref[s, :, pl.ds(n * 1024 + col, LANES)] for n in range(4)]
+    for d in range(32):
+        out_ref[d, ROWS:MSG, :] = labels
+
+    def step(s, carry):
+        station(s).wait()
+        rows = pl.ds(pl.multiple_of(s * WIN, WIN), WIN)
+        for q in range(8):
+            tiles = [x_ref[s, :, n * 1024 + q * LANES:n * 1024 + (q + 1) * LANES] for n in range(4)]
             for m, tile in enumerate(chunk_transpose(tiles)):
-                out_ref[4 * q + m, s * WIN:(s + 1) * WIN, :] = tile
-        for m in range(4):
-            out_ref[4 * q + m, ROWS:MSG, :] = labels
+                out_ref[4 * q + m, rows, :] = tile
         return carry
 
-    lax.fori_loop(0, 8, step, 0)
+    lax.fori_loop(0, STA, step, 0)
 
 
 def slot_bins(count_ref, order_ref):
@@ -81,46 +88,62 @@
     return out
 
 
-def cross_kernel(own_ref, halo_ref, count_ref, order_ref, out_ref, c_ref, t_ref, f_ref, x_ref, hot_ref):
+def joined(p, q):
+    low = lane_iota(p.shape) < 64
+    return jnp.where(low, p, q) + pltpu.roll(jnp.where(low, q, p), 64, 1)
+
+
+def cross_kernel(own_ref, count_ref, order_ref, out_ref, edge_hot_ref, c_ref, t_ref, f_ref, x_ref, hot_ref):
     lane = lane_iota((8, LANES))
     low = lane < 64
     zero = jnp.zeros((8, LANES), F32)
 
     spread = jnp.where(lax.broadcasted_iota(jnp.int32, (LANES, KI), 1) // 8
                        == lax.broadcasted_iota(jnp.int32, (LANES, KI), 0), 1.0, 0.0)
-    qmod = lax.broadcasted_iota(jnp.int32, (8, KI), 1) % 8
+    lane_q = lane_iota((8, KI))
+    qmod = lane_q % 8
     labels = jnp.zeros((8, KI), F32)
     for b in range(PLANE):
         wide = jnp.dot(own_ref[b * NG, ROWS:MSG, :].astype(F32), spread, preferred_element_type=F32)
         labels = labels + jnp.where(qmod == b, wide, 0.0)
+    labels = jnp.where(lane_q // 64 > qmod, -2.0, labels)
+
+    col = lane_iota((LANES, LANES))
+    row = lax.broadcasted_iota(jnp.int32, (LANES, LANES), 0)
+    variant, half, station = col // 64, (col % 8) // 4, (col // 8) % 8
+    first = jnp.where((variant == 0) & (row == (1 + half) * 8 + station), 1.0, 0.0).astype(F32)
+    second = jnp.where((variant == 1) & (row == 2 * 8 + station), 1.0, 0.0).astype(F32)
+    edge = jnp.dot(own_ref[0, ROWS:MSG, :].astype(F32), first, preferred_element_type=F32)
+    edge = edge + jnp.dot(own_ref[NG, ROWS:MSG, :].astype(F32), second, preferred_element_type=F32)
+    lane_e = lane_iota((8, LANES))
+    edge = jnp.where((lane_e >= 64) & (lane_e % 8 >= 4), -2.0, edge)
+
     bins = [jnp.broadcast_to(v, (64, KI)) for v in slot_bins(count_ref, order_ref)]
     for i in range(STA):
         row = jnp.broadcast_to(labels[i:i + 1, :], (64, KI))
+        edge_row = jnp.broadcast_to(edge[i:i + 1, :], (64, LANES))
         for k in range(CAP):
-            hot_ref[k * 64:(k + 1) * 64, i * KI:(i + 1) * KI] = jnp.where(bins[k] == row, 1.0, 0.0).astype(BF16)
+            rows = slice(k * 64, (k + 1) * 64)
+            hot_ref[rows, i * KI:(i + 1) * KI] = jnp.where(bins[k] == row, 1.0, 0.0).astype(BF16)
+            edge_hot_ref[rows, i * LANES:(i + 1) * LANES] = jnp.where(
+                bins[k][:, :LANES] == edge_row, 1.0, 0.0).astype(BF16)
 
     for i in range(STA):
         f_ref[i, STA * 8:(STA + 1) * 8, :] = zero
         x_ref[i * KI + ROUNDS * 64:(i + 1) * KI, :] = jnp.zeros((64, NG * LANES), BF16)
+        c_ref[i, 0:2 * PITCH, :] = jnp.zeros((2 * PITCH, LANES), F32)
 
     def per_shard(g, carry):
         sign = jnp.where(lane_iota((ROWS, LANES)) < 64, 1.0, -1.0).astype(F32)
-        for bb in range(PLANE + 2):
-            if bb < 2:
-                piece = halo_ref[bb * NG + g, 0:ROWS, :].astype(F32)
-            else:
-                piece = own_ref[(bb - 2) * NG + g, 0:ROWS, :].astype(F32)
-                turned = pltpu.roll(piece, 64, 1) * sign
+        for b in range(PLANE):
+            piece = own_ref[b * NG + g, 0:ROWS, :].astype(F32)
+            turned = pltpu.roll(piece, 64, 1) * sign
             for s in range(STA):
                 rows = slice(s * WIN, (s + 1) * WIN)
-                c_ref[s, bb * PITCH:bb * PITCH + WIN, :] = piece[rows]
-                if bb >= 2:
-                    t_ref[s, (bb - 2) * PITCH:(bb - 2) * PITCH + WIN, :] = turned[rows]
+                c_ref[s, (b + 2) * PITCH:(b + 2) * PITCH + WIN, :] = piece[rows]
+                t_ref[s, b * PITCH:b * PITCH + WIN, :] = turned[rows]
 
         lanes = pl.ds(pl.multiple_of(g * LANES, LANES), LANES)
-
-        def joined(p, q):
-            return jnp.where(low, p, q) + pltpu.roll(jnp.where(low, q, p), 64, 1)
 
         def row_of(i, r, others):
             p, q = {}, {}
@@ -157,7 +180,53 @@
 
     lax.fori_loop(0, NG, per_shard, 0)
     total = jnp.dot(hot_ref[...], x_ref[...], preferred_element_type=F32)
-    total = (total[:, 0:128] + total[:, 128:256]) + (total[:, 256:384] + total[:, 384:512])
+    out_ref[...] = (total[:, 0:128] + total[:, 128:256]) + (total[:, 256:384] + total[:, 384:512])
+
+
+def edge_kernel(own_ref, halo_ref, part_ref, hot_ref, out_ref, a_ref, t_ref, c_ref, x_ref):
+    sign = jnp.where(lane_iota((ROWS, LANES)) < 64, 1.0, -1.0).astype(F32)
+    zero = jnp.zeros((8, LANES), F32)
+    for g in range(NG):
+        for slot, (ref, index) in enumerate(((own_ref, g), (own_ref, NG + g), (halo_ref, NG + g), (halo_ref, g))):
+            piece = ref[index, 0:ROWS, :].astype(F32)
+            for s in range(STA):
+                rows = piece[s * WIN:(s + 1) * WIN]
+                if slot >= 2:
+                    base = ((slot - 2) * 4 + g) * PITCH
+                    c_ref[s, base:base + WIN, :] = rows
+                else:
+                    for half in range(2):
+                        base = (slot * 8 + half * 4 + g) * PITCH
+                        a_ref[s, base:base + WIN, :] = rows
+            if slot < 2:
+                turned = pltpu.roll(piece, 64, 1) * sign
+                for s in range(STA):
+                    for half in range(2):
+                        base = (slot * 8 + half * 4 + g) * PITCH
+                        t_ref[s, base:base + WIN, :] = turned[s * WIN:(s + 1) * WIN]
+
+    def per_station(i, carry):
+        for variant in range(2):
+            p, q = {}, {}
+            for w in range(WIN):
+                a = a_ref[i, pl.ds(variant * 8 * PITCH + w, 8, stride=PITCH), :]
+                t = t_ref[i, pl.ds(variant * 8 * PITCH + w, 8, stride=PITCH), :]
+                for j in range(STA):
+                    c = c_ref[j, pl.ds(w, 8, stride=PITCH), :]
+                    v = a * c
+                    p[j] = v if w == 0 else p[j] + v
+                    v = t * c
+                    q[j] = v if w == 0 else q[j] + v
+            values = [joined(p[j], q[j]) for j in range(STA)] + [zero]
+            for j in range(0, 8, 2):
+                pair = jnp.concatenate([values[j], values[j + 1]], axis=0).astype(BF16)
+                x_ref[i, (variant * 8 + j) * 8:(variant * 8 + j + 2) * 8, :] = pair
+        return carry
+
+    lax.fori_loop(0, STA, per_station, 0)
+    total = part_ref[...]
+    for i in range(STA):
+        total = total + jnp.dot(hot_ref[:, i * LANES:(i + 1) * LANES], x_ref[i], preferred_element_type=F32)
     for w, tile in enumerate(chunk_transpose([total[k * 64:(k + 1) * 64, :] for k in range(CAP)])):
         out_ref[pl.ds(w, 64, stride=4), :] = tile
 
@@ -177,19 +246,21 @@
     vmem = pl.BlockSpec(memory_space=pltpu.VMEM)
     packed = pl.pallas_call(
         pack_kernel,
-        out_shape=jax.ShapeDtypeStruct((32, MSG, LANES), BF16),
-        in_specs=[vmem, vmem],
+        out_shape=pltpu.VMEM((32, MSG, LANES), BF16),
+        in_specs=[pl.BlockSpec(memory_space=pl.ANY), vmem],
         out_specs=vmem,
+        scratch_shapes=[pltpu.VMEM((STA, WIN, 4096), BF16), pltpu.SemaphoreType.DMA((STA,))],
         name="pack",
     )(jnp.transpose(spectra, (1, 0, 2)), jnp.transpose(pair_bins, (1, 0, 2)))
     own = lax.all_to_all(packed, ("y", "c", "win"), 0, 0)
     count = lax.axis_size("z")
     halo = lax.ppermute(own[24:32], "z", [(i, (i + 1) % count) for i in range(count)])
-    send = pl.pallas_call(
+    own = pltpu.with_memory_space_constraint(own, pltpu.VMEM)
+    part, edge_hot = pl.pallas_call(
         cross_kernel,
-        out_shape=jax.ShapeDtypeStruct((256, LANES), F32),
-        in_specs=[vmem] * 4,
-        out_specs=vmem,
+        out_shape=(pltpu.VMEM((256, LANES), F32), pltpu.VMEM((256, STA * LANES), BF16)),
+        in_specs=[vmem] * 3,
+        out_specs=(vmem, vmem),
         scratch_shapes=[
             pltpu.VMEM((STA, 176, LANES), F32),
             pltpu.VMEM((STA, 144, LANES), F32),
@@ -198,8 +269,23 @@
             pltpu.VMEM((256, STA * KI), BF16),
         ],
         name="cross",
-    )(own, halo, owner_count.reshape(1, -1), bin_order.reshape(1, -1))
+    )(own, owner_count.reshape(1, -1), bin_order.reshape(1, -1))
+    halo = pltpu.with_memory_space_constraint(halo, pltpu.VMEM)
+    send = pl.pallas_call(
+        edge_kernel,
+        out_shape=pltpu.VMEM((256, LANES), F32),
+        in_specs=[vmem] * 4,
+        out_specs=vmem,
+        scratch_shapes=[
+            pltpu.VMEM((STA, 16 * PITCH, LANES), F32),
+            pltpu.VMEM((STA, 16 * PITCH, LANES), F32),
+            pltpu.VMEM((STA, 8 * PITCH, LANES), F32),
+            pltpu.VMEM((STA, LANES, LANES), BF16),
+        ],
+        name="edge",
+    )(own, halo, *(pltpu.with_memory_space_constraint(v, pltpu.VMEM) for v in (part, edge_hot)))
     got = lax.all_to_all(send.reshape(256, 1, LANES), ("z", "y", "c", "win"), 0, 0)
+    got = pltpu.with_memory_space_constraint(got.reshape(8, 32, LANES), pltpu.VMEM)
     return pl.pallas_call(
         finish_kernel,
         out_shape=jax.ShapeDtypeStruct((CAP, 1024), F32),
@@ -207,7 +293,7 @@
         out_specs=vmem,
         scratch_shapes=[pltpu.VMEM((32, LANES), F32)],
         name="finish",
-    )(got.reshape(8, 32, LANES))
+    )(got)
 
 
 def solution(mesh):

time: 73.5 us -> 63.9 us (0.87)
  waiting for transfers between devices: 9.1 us -> 1.17 us
  Pallas kernels: 14.7 us -> 13.9 us
    ppermute x1, waiting for transfers between devices: 9.1 us -> 1.17 us  [on_device(): lax.ppermute(own[24:32], 'z', [(i, (i + 1) % count) for i in range(count)])]
    pallas_call x1, Pallas kernels: 1.67 us -> 0.77 us  [on_device(): pl.pallas_call(finish_kernel, out_shape=jax.ShapeDtypeStruct((CAP, 1024),...]
    pallas_call x2 -> x3, Pallas kernels: 13.1 us -> 13.1 us  [the longest x1 7.92 us: on_device(): pl.pallas_call(cross_kernel, out_shape=(pltpu.VMEM((256, LANES), F32), pl...]
  transfers between devices with their start and end apart: 1 -> 1, of which waited for: 1 -> 1; matrix products, arithmetic and copies ran while one was open for 0% -> 0% of each run, Pallas kernels for 0% -> 12%
where the time goes in v2:
time: 63.9 us; the launch traced here: 63.7 us
  blocking collectives  46.8 us (73%)
  Pallas kernels  13.9 us (22%)
  starting transfers between devices  1.71 us (3%)
  waiting for transfers between devices  1.17 us (2%)
    all_to_all x1, blocking collectives, on_device(): own = lax.all_to_all(packed, ('y', 'c', 'win'), 0, 0)  23.8 us
    all_to_all x1, blocking collectives, on_device(): lax.all_to_all(send.reshape(256, 1, LANES), ('z', 'y', 'c', 'win'), 0, 0)  23 us
    pallas_call x1, Pallas kernels, on_device(): pl.pallas_call(cross_kernel, out_shape=(pltpu.VMEM((256, LANES), F32), pl...  7.92 us
    pallas_call x1, Pallas kernels, on_device(): pl.pallas_call(pack_kernel, out_shape=pltpu.VMEM((32, MSG, LANES), BF16),...  3 us
    pallas_call x1, Pallas kernels, on_device(): pl.pallas_call(edge_kernel, out_shape=pltpu.VMEM((256, LANES), F32), in_s...  2.23 us
    ppermute x1, starting transfers between devices, on_device(): lax.ppermute(own[24:32], 'z', [(i, (i + 1) % count) for i in range(count)])  1.71 us
  transfers between devices with their start and end apart: 1, of which 1 were waited for; matrix products, arithmetic and copies ran while one was open for 0% of the time, Pallas kernels for 12%

profile of v2, /device:TPU:1, one launch (start us, length us, event | category | flops | bytes accessed | tf_op | source)
XLA Modules:
  0.0 63.7 jit_solution(6778329152188267416)
XLA Ops:
  0.0 3.0 %pack.1 = bf16[32,120,128]{2,1,0:T(8,128)(2,1)S(1)} custom-call(bf16[7,16,4096]{2,1,0:T(8,128)(2,1)} %bitcast.10, s32[3,7,7]{2,1,0:T(8,128)} %bitcast.11), custom_call_target="tpu_custom_call" | custom-call | tf_op jit(solution)/shard_map/pack/pallas_call | solution.py:247
  3.0 23.8 %all_to_all.10.own_ref = bf16[32,120,128]{2,1,0:T(8,128)(2,1)S(1)} all-to-all(bf16[32,120,128]{2,1,0:T(8,128)(2,1)S(1)} %pack.1), channel_id=1, replica_groups=mesh['z'=8,'y'=4,'c'=2,'win'=4] {'y','c','win'}, dimensions={0} | all-to-all | bytes 1966080 | tf_op jit(solution)/shard_map/all_to_all | solution.py:255
  26.9 1.7 %collective-permute-start = (bf16[8,120,128]{2,1,0:T(8,128)(2,1)S(1)}, bf16[8,120,128]{2,1,0:T(8,128)(2,1)S(1)}, u32[]{:S(2)}, u32[]{:S(2)}) collective-permute-start(bf16[8,120,128]{2,1,0:T(8,128)(2,1)S(1)} %slice.4), channel_id=1, source_target_pairs={{0,32},{32,64},{64,96},{96,128},{128,160},{160,192},{192,224},{224... | collective-permute-start | bytes 737288 | tf_op jit(solution)/shard_map/ppermute | solution.py:257
  28.6 7.9 %cross.1 = (f32[256,128]{1,0:T(8,128)S(1)}, bf16[256,896]{1,0:T(8,128)(2,1)S(1)}) custom-call(bf16[32,120,128]{2,1,0:T(8,128)(2,1)S(1)} %all_to_all.10.own_ref, s32[1,64]{1,0:T(1,128)} %bitcast.12, s32[1,128]{1,0:T(1,128)} %bitcast.13), custom_call_target="tpu_custom_call" | custom-call | tf_op jit(solution)/shard_map/cross/pallas_call | solution.py:259
  36.5 1.2 %collective-permute-done.halo_ref = bf16[8,120,128]{2,1,0:T(8,128)(2,1)S(1)} collective-permute-done((bf16[8,120,128]{2,1,0:T(8,128)(2,1)S(1)}, bf16[8,120,128]{2,1,0:T(8,128)(2,1)S(1)}, u32[]{:S(2)}, u32[]{:S(2)}) %collective-permute-start) | collective-permute-done | bytes 245792 | tf_op jit(solution)/shard_map/ppermute | solution.py:257
  37.7 2.2 %edge.1 = f32[256,128]{1,0:T(8,128)S(1)} custom-call(bf16[32,120,128]{2,1,0:T(8,128)(2,1)S(1)} %all_to_all.10.own_ref, bf16[8,120,128]{2,1,0:T(8,128)(2,1)S(1)} %collective-permute-done.halo_ref, f32[256,128]{1,0:T(8,128)S(1)} %get-tuple-element.7.part_ref, bf16[256,896]{1,0:T(8,128)(2,1)S(1)} %get-tuple-element.8.hot_ref), custom_call_target="tpu_custom_call" | custom-call | tf_op jit(solution)/shard_map/edge/pallas_call | solution.py:274
  39.9 23.0 %all_to_all.11 = f32[256,1,128]{2,1,0:T(1,128)S(1)} all-to-all(f32[256,1,128]{2,1,0:T(1,128)S(1)} %bitcast.9), channel_id=1, replica_groups=mesh['z'=8,'y'=4,'c'=2,'win'=4] {'z','y','c','win'}, dimensions={0} | all-to-all | bytes 262144 | tf_op jit(solution)/shard_map/all_to_all | solution.py:287
  62.9 0.8 %finish.1 = f32[4,1024]{1,0:T(4,128)} custom-call(f32[8,32,128]{2,1,0:T(8,128)S(1)} %bitcast.8), custom_call_target="tpu_custom_call" | custom-call | tf_op jit(solution)/shard_map/finish/pallas_call | solution.py:289
  (1 shorter events, 0.0 us)
Async XLA Ops:
  26.9 10.8 %collective-permute-start = (bf16[8,120,128]{2,1,0:T(8,128)(2,1)S(1)}, bf16[8,120,128]{2,1,0:T(8,128)(2,1)S(1)}, u32[]{:S(2)}, u32[]{:S(2)}) collective-permute-start(bf16[8,120,128]{2,1,0:T(8,128)(2,1)S(1)} %slice.4), channel_id=1, source_target_pairs={{0,32},{32,64},{64,96},{96,128},{128,160},{160,192},{192,224},{224... | collective-permute-start | bytes 737288 | tf_op jit(solution)/shard_map/ppermute | solution.py:257

commit v3 on v2

--- a/solution.py
+++ b/solution.py
@@ -44,12 +44,15 @@
     return v0, v1, v2, v3
 
 
-def pack_kernel(x_hbm, bins_ref, out_ref, x_ref, sems):
+def pack_kernel(x_hbm, bins_hbm, out_ref, x_ref, bins_ref, sems, bins_sem):
     def station(s):
         return pltpu.make_async_copy(x_hbm.at[s], x_ref.at[s], sems.at[s])
 
+    bins_copy = pltpu.make_async_copy(bins_hbm, bins_ref, bins_sem)
+    bins_copy.start()
     for s in range(STA):
         station(s).start()
+    bins_copy.wait()
     lane8 = lax.broadcasted_iota(jnp.int32, (STA, LANES), 1)
     row8 = lax.broadcasted_iota(jnp.int32, (STA, LANES), 0)
     labels = jnp.zeros((STA, LANES), F32)
@@ -57,7 +60,6 @@
         place = jnp.where(lane8 == row8 + 8 * r, 1.0, 0.0).astype(F32)
         labels = labels + jnp.dot(bins_ref[r].astype(F32), place, preferred_element_type=F32)
     labels = jnp.concatenate([labels, jnp.zeros((1, LANES), F32)], axis=0).astype(BF16)
-
     for d in range(32):
         out_ref[d, ROWS:MSG, :] = labels
 
@@ -93,7 +95,7 @@
     return jnp.where(low, p, q) + pltpu.roll(jnp.where(low, q, p), 64, 1)
 
 
-def cross_kernel(own_ref, count_ref, order_ref, out_ref, edge_hot_ref, c_ref, t_ref, f_ref, x_ref, hot_ref):
+def cross_kernel(own_ref, count_ref, order_ref, out_ref, edge_hot_ref, t_ref, s_ref, m_ref, e_ref, d_ref, f_ref, x_ref, hot_ref):
     lane = lane_iota((8, LANES))
     low = lane < 64
     zero = jnp.zeros((8, LANES), F32)
@@ -131,47 +133,75 @@
     for i in range(STA):
         f_ref[i, STA * 8:(STA + 1) * 8, :] = zero
         x_ref[i * KI + ROUNDS * 64:(i + 1) * KI, :] = jnp.zeros((64, NG * LANES), BF16)
-        c_ref[i, 0:2 * PITCH, :] = jnp.zeros((2 * PITCH, LANES), F32)
+        m_ref[i, 0:2 * PITCH, :] = jnp.zeros((2 * PITCH, LANES), F32)
 
     def per_shard(g, carry):
-        sign = jnp.where(lane_iota((ROWS, LANES)) < 64, 1.0, -1.0).astype(F32)
+        low_rows = lane_iota((ROWS, LANES)) < 64
+        before = [jnp.zeros((ROWS, LANES), F32)] * 2
+        turned_before = jnp.zeros((ROWS, LANES), F32)
         for b in range(PLANE):
             piece = own_ref[b * NG + g, 0:ROWS, :].astype(F32)
-            turned = pltpu.roll(piece, 64, 1) * sign
+            turned = pltpu.roll(piece, 64, 1)
+            total = piece + turned
+            mixed = jnp.where(low_rows, piece - turned, total)
+            shared = jnp.where(low_rows, before[0], before[1])
             for s in range(STA):
                 rows = slice(s * WIN, (s + 1) * WIN)
-                c_ref[s, (b + 2) * PITCH:(b + 2) * PITCH + WIN, :] = piece[rows]
-                t_ref[s, b * PITCH:b * PITCH + WIN, :] = turned[rows]
+                own_rows = slice(b * PITCH, b * PITCH + WIN)
+                t_ref[s, own_rows, :] = turned[rows]
+                s_ref[s, own_rows, :] = total[rows]
+                m_ref[s, (b + 2) * PITCH:(b + 2) * PITCH + WIN, :] = mixed[rows]
+                e_ref[s, own_rows, :] = shared[rows]
+                if s % 2 == 1:
+                    d_ref[s // 2, own_rows, :] = jnp.where(
+                        low_rows[:WIN], piece[rows], turned[(s + 1) * WIN:(s + 2) * WIN])
+            before = [piece, turned_before]
+            turned_before = turned
 
         lanes = pl.ds(pl.multiple_of(g * LANES, LANES), LANES)
 
-        def row_of(i, r, others):
-            p, q = {}, {}
+        def add(acc, key, w, v):
+            acc[key] = v if w == 0 else acc[key] + v
+
+        def spread_of(k):
+            turned = pltpu.roll(k, 64, 1)
+            return jnp.where(low, k, turned), jnp.where(low, turned, k)
+
+        for i in range(STA):
+            k1, k1_own, k23 = {}, {}, {}
+            pairs = [n for n in range(3) if 2 * n + 2 > i]
             for w in range(WIN):
-                a = c_ref[i, pl.ds(2 * PITCH + w, 8, stride=PITCH), :]
-                t = t_ref[i, pl.ds(w, 8, stride=PITCH), :]
-                for j in others:
-                    if r == 0 and j == i:
-                        v = a * a
-                        p[j] = v if w == 0 else p[j] + v
-                        continue
-                    c = c_ref[j, pl.ds((2 - r) * PITCH + w, 8, stride=PITCH), :]
-                    v = a * c
-                    p[j] = v if w == 0 else p[j] + v
-                    v = t * c
-                    q[j] = v if w == 0 else q[j] + v
-            return {j: joined(p[j], q.get(j, zero)) for j in others}
-
-        for i in range(STA):
-            for j, value in row_of(i, 0, list(range(i, STA))).items():
-                f_ref[i, j * 8:(j + 1) * 8, :] = value
-                if j != i:
-                    f_ref[j, i * 8:(i + 1) * 8, :] = jnp.where(low, value, -value)
+                rows = pl.ds(w, 8, stride=PITCH)
+                t = t_ref[i, rows, :]
+                total = s_ref[i, rows, :]
+                add(k23, (0, i), w, t * t)
+                for j in range(i + 1, STA):
+                    add(k23, (0, j), w, t * m_ref[j, pl.ds(2 * PITCH + w, 8, stride=PITCH), :])
+                for n in pairs:
+                    add(k1_own, n, w, total * d_ref[n, rows, :])
+            auto = k23[0, i]
+            f_ref[i, i * 8:(i + 1) * 8, :] = jnp.where(low, auto + pltpu.roll(auto, 64, 1), 0.0)
+            for n in pairs:
+                for j, k in zip((2 * n + 1, 2 * n + 2), spread_of(k1_own[n])):
+                    if j > i:
+                        value = k - k23[0, j]
+                        f_ref[i, j * 8:(j + 1) * 8, :] = value
+                        f_ref[j, i * 8:(i + 1) * 8, :] = jnp.where(low, value, -value)
+            for w in range(WIN):
+                rows = pl.ds(w, 8, stride=PITCH)
+                t = t_ref[i, rows, :]
+                total = s_ref[i, rows, :]
+                for j in range(STA):
+                    add(k23, (1, j), w, t * m_ref[j, pl.ds(PITCH + w, 8, stride=PITCH), :])
+                    add(k23, (2, j), w, t * m_ref[j, rows, :])
+                    add(k1, j, w, total * e_ref[j, rows, :])
+            values = {(1, STA): zero, (2, STA): zero}
+            for j in range(STA):
+                for r, k in zip((1, 2), spread_of(k1[j])):
+                    values[r, j] = k - k23[r, j]
             for r in (1, 2):
-                values = row_of(i, r, list(range(STA)))
-                values[STA] = zero
                 for j in range(0, 8, 2):
-                    pair = jnp.concatenate([values[j], values[j + 1]], axis=0).astype(BF16)
+                    pair = jnp.concatenate([values[r, j], values[r, j + 1]], axis=0).astype(BF16)
                     base = i * KI + (r * 8 + j) * 8
                     x_ref[base:base + 16, lanes] = pair
         for i in range(STA):
@@ -242,35 +272,47 @@
             out_ref[k:k + 1, t * LANES:(t + 1) * LANES] = tiles[k][t:t + 1, :]
 
 
+def in_vmem(value):
+    return pltpu.with_memory_space_constraint(value, pltpu.VMEM)
+
+
 def on_device(spectra, pair_bins, owner_count, bin_order):
     vmem = pl.BlockSpec(memory_space=pltpu.VMEM)
     packed = pl.pallas_call(
         pack_kernel,
         out_shape=pltpu.VMEM((32, MSG, LANES), BF16),
-        in_specs=[pl.BlockSpec(memory_space=pl.ANY), vmem],
+        in_specs=[pl.BlockSpec(memory_space=pl.ANY)] * 2,
         out_specs=vmem,
-        scratch_shapes=[pltpu.VMEM((STA, WIN, 4096), BF16), pltpu.SemaphoreType.DMA((STA,))],
+        scratch_shapes=[
+            pltpu.VMEM((STA, WIN, 4096), BF16),
+            pltpu.VMEM((ROUNDS, STA, STA), jnp.int32),
+            pltpu.SemaphoreType.DMA((STA,)),
+            pltpu.SemaphoreType.DMA,
+        ],
         name="pack",
     )(jnp.transpose(spectra, (1, 0, 2)), jnp.transpose(pair_bins, (1, 0, 2)))
     own = lax.all_to_all(packed, ("y", "c", "win"), 0, 0)
     count = lax.axis_size("z")
     halo = lax.ppermute(own[24:32], "z", [(i, (i + 1) % count) for i in range(count)])
-    own = pltpu.with_memory_space_constraint(own, pltpu.VMEM)
+    own = in_vmem(own)
     part, edge_hot = pl.pallas_call(
         cross_kernel,
         out_shape=(pltpu.VMEM((256, LANES), F32), pltpu.VMEM((256, STA * LANES), BF16)),
         in_specs=[vmem] * 3,
         out_specs=(vmem, vmem),
         scratch_shapes=[
+            pltpu.VMEM((STA, 144, LANES), F32),
+            pltpu.VMEM((STA, 144, LANES), F32),
             pltpu.VMEM((STA, 176, LANES), F32),
             pltpu.VMEM((STA, 144, LANES), F32),
+            pltpu.VMEM((3, 144, LANES), F32),
             pltpu.VMEM((STA, 64, LANES), F32),
             pltpu.VMEM((STA * KI, NG * LANES), BF16),
             pltpu.VMEM((256, STA * KI), BF16),
         ],
         name="cross",
-    )(own, owner_count.reshape(1, -1), bin_order.reshape(1, -1))
-    halo = pltpu.with_memory_space_constraint(halo, pltpu.VMEM)
+    )(own, in_vmem(owner_count.reshape(1, -1)), in_vmem(bin_order.reshape(1, -1)))
+    halo = in_vmem(halo)
     send = pl.pallas_call(
         edge_kernel,
         out_shape=pltpu.VMEM((256, LANES), F32),
@@ -283,9 +325,9 @@
             pltpu.VMEM((STA, LANES, LANES), BF16),
         ],
         name="edge",
-    )(own, halo, *(pltpu.with_memory_space_constraint(v, pltpu.VMEM) for v in (part, edge_hot)))
+    )(own, halo, in_vmem(part), in_vmem(edge_hot))
     got = lax.all_to_all(send.reshape(256, 1, LANES), ("z", "y", "c", "win"), 0, 0)
-    got = pltpu.with_memory_space_constraint(got.reshape(8, 32, LANES), pltpu.VMEM)
+    got = in_vmem(got.reshape(8, 32, LANES))
     return pl.pallas_call(
         finish_kernel,
         out_shape=jax.ShapeDtypeStruct((CAP, 1024), F32),

time: 63.9 us -> 63 us (0.986)
  Pallas kernels: 13.9 us -> 11.6 us
  waiting for transfers between devices: 1.17 us -> 2.4 us
  local copies, waits for them, and re-layouts: 0.02 us -> 0.69 us
    pallas_call x1, Pallas kernels: 7.92 us -> 6.02 us  [on_device(): pl.pallas_call(cross_kernel, out_shape=(pltpu.VMEM((256, LANES), F32), pl...]
    ppermute x1, waiting for transfers between devices: 1.17 us -> 2.4 us  [on_device(): lax.ppermute(own[24:32], 'z', [(i, (i + 1) % count) for i in range(count)])]
    unnamed x0 -> x4, local copies, waits for them, and re-layouts: none -> 0.67 us
  transfers between devices with their start and end apart: 1 -> 1, of which waited for: 1 -> 1; matrix products, arithmetic and copies ran while one was open for 0% -> 0% of each run, Pallas kernels for 12% -> 10%
where the time goes in v3:
time: 63 us; the launch traced here: 62.8 us
  blocking collectives  46.4 us (74%)
  Pallas kernels  11.6 us (18%)
  waiting for transfers between devices  2.4 us (4%)
  starting transfers between devices  1.71 us (3%)
  local copies, waits for them, and re-layouts  0.69 us (1%)
    all_to_all x1, blocking collectives, on_device(): own = lax.all_to_all(packed, ('y', 'c', 'win'), 0, 0)  23.8 us
    all_to_all x1, blocking collectives, on_device(): lax.all_to_all(send.reshape(256, 1, LANES), ('z', 'y', 'c', 'win'), 0, 0)  22.6 us
    pallas_call x1, Pallas kernels, on_device(): pl.pallas_call(cross_kernel, out_shape=(pltpu.VMEM((256, LANES), F32), pl...  6.02 us
    pallas_call x1, Pallas kernels, on_device(): pl.pallas_call(pack_kernel, out_shape=pltpu.VMEM((32, MSG, LANES), BF16),...  2.56 us
    ppermute x1, waiting for transfers between devices, on_device(): lax.ppermute(own[24:32], 'z', [(i, (i + 1) % count) for i in range(count)])  2.4 us
    pallas_call x1, Pallas kernels, on_device(): pl.pallas_call(edge_kernel, out_shape=pltpu.VMEM((256, LANES), F32), in_s...  2.23 us
    ppermute x1, starting transfers between devices, on_device(): lax.ppermute(own[24:32], 'z', [(i, (i + 1) % count) for i in range(count)])  1.71 us
  transfers between devices with their start and end apart: 1, of which 1 were waited for; matrix products, arithmetic and copies ran while one was open for 0% of the time, Pallas kernels for 10%

profile of v3, /device:TPU:1, one launch (start us, length us, event | category | flops | bytes accessed | tf_op | source)
XLA Modules:
  0.0 62.8 jit_solution(5337747026655005273)
XLA Ops:
  0.0 2.6 %pack.1 = bf16[32,120,128]{2,1,0:T(8,128)(2,1)S(1)} custom-call(bf16[7,16,4096]{2,1,0:T(8,128)(2,1)} %bitcast.12, s32[3,7,7]{2,1,0:T(8,128)} %bitcast.13), custom_call_target="tpu_custom_call" | custom-call | tf_op jit(solution)/shard_map/pack/pallas_call | solution.py:281
  2.6 23.8 %all_to_all.10.own_ref = bf16[32,120,128]{2,1,0:T(8,128)(2,1)S(1)} all-to-all(bf16[32,120,128]{2,1,0:T(8,128)(2,1)S(1)} %pack.1), channel_id=1, replica_groups=mesh['z'=8,'y'=4,'c'=2,'win'=4] {'y','c','win'}, dimensions={0} | all-to-all | bytes 1966080 | tf_op jit(solution)/shard_map/all_to_all | solution.py:294
  26.4 1.7 %collective-permute-start = (bf16[8,120,128]{2,1,0:T(8,128)(2,1)S(1)}, bf16[8,120,128]{2,1,0:T(8,128)(2,1)S(1)}, u32[]{:S(2)}, u32[]{:S(2)}) collective-permute-start(bf16[8,120,128]{2,1,0:T(8,128)(2,1)S(1)} %slice.4), channel_id=1, source_target_pairs={{0,32},{32,64},{64,96},{96,128},{128,160},{160,192},{192,224},{224... | collective-permute-start | bytes 737288 | tf_op jit(solution)/shard_map/ppermute | solution.py:296
  28.1 0.0 copy-start
  28.1 0.0 copy-start.1
  28.1 0.7 %copy-done = s32[64]{0:T(128)S(1)} copy-done((s32[64]{0:T(128)S(1)}, s32[64]{0:T(128)}, u32[]{:S(2)}) %copy-start) | copy-done | bytes 280
  28.8 0.0 copy-done.1
  28.8 6.0 %cross.1 = (f32[256,128]{1,0:T(8,128)S(1)}, bf16[256,896]{1,0:T(8,128)(2,1)S(1)}) custom-call(bf16[32,120,128]{2,1,0:T(8,128)(2,1)S(1)} %all_to_all.10.own_ref, s32[1,64]{1,0:T(1,128)S(1)} %bitcast.10, s32[1,128]{1,0:T(1,128)S(1)} %bitcast.11), custom_call_target="tpu_custom_call" | custom-call | tf_op jit(solution)/shard_map/cross/pallas_call | solution.py:298
  34.8 2.4 %collective-permute-done.halo_ref = bf16[8,120,128]{2,1,0:T(8,128)(2,1)S(1)} collective-permute-done((bf16[8,120,128]{2,1,0:T(8,128)(2,1)S(1)}, bf16[8,120,128]{2,1,0:T(8,128)(2,1)S(1)}, u32[]{:S(2)}, u32[]{:S(2)}) %collective-permute-start) | collective-permute-done | bytes 245792 | tf_op jit(solution)/shard_map/ppermute | solution.py:296
  37.2 2.2 %edge.1 = f32[256,128]{1,0:T(8,128)S(1)} custom-call(bf16[32,120,128]{2,1,0:T(8,128)(2,1)S(1)} %all_to_all.10.own_ref, bf16[8,120,128]{2,1,0:T(8,128)(2,1)S(1)} %collective-permute-done.halo_ref, f32[256,128]{1,0:T(8,128)S(1)} %get-tuple-element.7.part_ref, bf16[256,896]{1,0:T(8,128)(2,1)S(1)} %get-tuple-element.8.hot_ref), custom_call_target="tpu_custom_call" | custom-call | tf_op jit(solution)/shard_map/edge/pallas_call | solution.py:316
  39.5 22.6 %all_to_all.11 = f32[256,1,128]{2,1,0:T(1,128)S(1)} all-to-all(f32[256,1,128]{2,1,0:T(1,128)S(1)} %bitcast.9), channel_id=1, replica_groups=mesh['z'=8,'y'=4,'c'=2,'win'=4] {'z','y','c','win'}, dimensions={0} | all-to-all | bytes 262144 | tf_op jit(solution)/shard_map/all_to_all | solution.py:329
  62.0 0.8 %finish.1 = f32[4,1024]{1,0:T(4,128)} custom-call(f32[8,32,128]{2,1,0:T(8,128)S(1)} %bitcast.8), custom_call_target="tpu_custom_call" | custom-call | tf_op jit(solution)/shard_map/finish/pallas_call | solution.py:331
  (1 shorter events, 0.0 us)
Async XLA Ops:
  26.4 10.8 %collective-permute-start = (bf16[8,120,128]{2,1,0:T(8,128)(2,1)S(1)}, bf16[8,120,128]{2,1,0:T(8,128)(2,1)S(1)}, u32[]{:S(2)}, u32[]{:S(2)}) collective-permute-start(bf16[8,120,128]{2,1,0:T(8,128)(2,1)S(1)} %slice.4), channel_id=1, source_target_pairs={{0,32},{32,64},{64,96},{96,128},{128,160},{160,192},{192,224},{224... | collective-permute-start | bytes 737288 | tf_op jit(solution)/shard_map/ppermute | solution.py:296
  28.1 0.7 %copy-start = (s32[64]{0:T(128)S(1)}, s32[64]{0:T(128)}, u32[]{:S(2)}) copy-start(s32[64]{0:T(128)} %param.6) | copy-start | bytes 772
  28.1 0.7 %copy-start.1 = (s32[128]{0:T(128)S(1)}, s32[128]{0:T(128)}, u32[]{:S(2)}) copy-start(s32[128]{0:T(128)} %param.7) | copy-start | bytes 1540

commit v4 on v3

--- a/solution.py
+++ b/solution.py
@@ -17,6 +17,7 @@
 LANES = 128
 CHUNK = 32
 KI = 256
+SMALL = pltpu.CompilerParams(vmem_limit_bytes=16 << 20)
 F32 = jnp.float32
 BF16 = jnp.bfloat16
 
@@ -44,14 +45,18 @@
     return v0, v1, v2, v3
 
 
-def pack_kernel(x_hbm, bins_hbm, out_ref, x_ref, bins_ref, sems, bins_sem):
+def pack_kernel(x_hbm, bins_hbm, count_hbm, order_hbm, out_ref, count_ref, order_ref, x_ref, bins_ref, sems, small_sems):
     def station(s):
         return pltpu.make_async_copy(x_hbm.at[s], x_ref.at[s], sems.at[s])
 
-    bins_copy = pltpu.make_async_copy(bins_hbm, bins_ref, bins_sem)
+    bins_copy = pltpu.make_async_copy(bins_hbm, bins_ref, small_sems.at[0])
+    count_copy = pltpu.make_async_copy(count_hbm, count_ref, small_sems.at[1])
+    order_copy = pltpu.make_async_copy(order_hbm, order_ref, small_sems.at[2])
     bins_copy.start()
     for s in range(STA):
         station(s).start()
+    count_copy.start()
+    order_copy.start()
     bins_copy.wait()
     lane8 = lax.broadcasted_iota(jnp.int32, (STA, LANES), 1)
     row8 = lax.broadcasted_iota(jnp.int32, (STA, LANES), 0)
@@ -73,6 +78,8 @@
         return carry
 
     lax.fori_loop(0, STA, step, 0)
+    count_copy.wait()
+    order_copy.wait()
 
 
 def slot_bins(count_ref, order_ref):
@@ -95,40 +102,54 @@
     return jnp.where(low, p, q) + pltpu.roll(jnp.where(low, q, p), 64, 1)
 
 
-def cross_kernel(own_ref, count_ref, order_ref, out_ref, edge_hot_ref, t_ref, s_ref, m_ref, e_ref, d_ref, f_ref, x_ref, hot_ref):
+def spread_of(k):
+    low = lane_iota(k.shape) < 64
+    turned = pltpu.roll(k, 64, 1)
+    return jnp.where(low, k, turned), jnp.where(low, turned, k)
+
+
+def cross_kernel(own_ref, count_ref, order_ref, out_ref, edge_hot_ref, edge_t_ref, edge_s_ref,
+                 t_ref, s_ref, m_ref, e_ref, d_ref, f_ref, x_ref, hot_ref):
     lane = lane_iota((8, LANES))
     low = lane < 64
     zero = jnp.zeros((8, LANES), F32)
 
     spread = jnp.where(lax.broadcasted_iota(jnp.int32, (LANES, KI), 1) // 8
-                       == lax.broadcasted_iota(jnp.int32, (LANES, KI), 0), 1.0, 0.0)
+                       == lax.broadcasted_iota(jnp.int32, (LANES, KI), 0), 1.0, 0.0).astype(BF16)
     lane_q = lane_iota((8, KI))
     qmod = lane_q % 8
     labels = jnp.zeros((8, KI), F32)
     for b in range(PLANE):
-        wide = jnp.dot(own_ref[b * NG, ROWS:MSG, :].astype(F32), spread, preferred_element_type=F32)
+        wide = jnp.dot(own_ref[b * NG, ROWS:MSG, :], spread, preferred_element_type=F32)
         labels = labels + jnp.where(qmod == b, wide, 0.0)
     labels = jnp.where(lane_q // 64 > qmod, -2.0, labels)
+    rows_of = [labels[i:i + 1, h * LANES:(h + 1) * LANES] for i in range(STA) for h in range(2)]
 
     col = lane_iota((LANES, LANES))
     row = lax.broadcasted_iota(jnp.int32, (LANES, LANES), 0)
-    variant, half, station = col // 64, (col % 8) // 4, (col // 8) % 8
-    first = jnp.where((variant == 0) & (row == (1 + half) * 8 + station), 1.0, 0.0).astype(F32)
-    second = jnp.where((variant == 1) & (row == 2 * 8 + station), 1.0, 0.0).astype(F32)
-    edge = jnp.dot(own_ref[0, ROWS:MSG, :].astype(F32), first, preferred_element_type=F32)
-    edge = edge + jnp.dot(own_ref[NG, ROWS:MSG, :].astype(F32), second, preferred_element_type=F32)
-    lane_e = lane_iota((8, LANES))
-    edge = jnp.where((lane_e >= 64) & (lane_e % 8 >= 4), -2.0, edge)
-
-    bins = [jnp.broadcast_to(v, (64, KI)) for v in slot_bins(count_ref, order_ref)]
-    for i in range(STA):
-        row = jnp.broadcast_to(labels[i:i + 1, :], (64, KI))
-        edge_row = jnp.broadcast_to(edge[i:i + 1, :], (64, LANES))
-        for k in range(CAP):
-            rows = slice(k * 64, (k + 1) * 64)
-            hot_ref[rows, i * KI:(i + 1) * KI] = jnp.where(bins[k] == row, 1.0, 0.0).astype(BF16)
-            edge_hot_ref[rows, i * LANES:(i + 1) * LANES] = jnp.where(
-                bins[k][:, :LANES] == edge_row, 1.0, 0.0).astype(BF16)
+    half, station = (col % 8) // 4, (col % 64) // 8
+    first = jnp.where(row == (1 + half) * 8 + station, 1.0, 0.0).astype(BF16)
+    second = jnp.where(row == 2 * 8 + station, 1.0, 0.0).astype(BF16)
+    one = jnp.dot(own_ref[0, ROWS:MSG, :], first, preferred_element_type=F32)
+    two = jnp.dot(own_ref[NG, ROWS:MSG, :], second, preferred_element_type=F32)
+    none = lax.broadcasted_iota(jnp.int32, (8, LANES), 0) == STA
+    one = jnp.where(none, -2.0, one)
+    two = jnp.where(none, -2.0, two)
+    lane_1 = lane_iota((1, LANES))
+    upper, second_half = lane_1 >= 64, lane_1 % 8 >= 4
+    edge_rows = [jnp.where(upper, one[2 * p + 1:2 * p + 2], one[2 * p:2 * p + 1]) for p in range(4)]
+    for p in (0, 2):
+        lower_unit = jnp.where(second_half, two[2 * p + 1:2 * p + 2], two[2 * p:2 * p + 1])
+        upper_unit = jnp.where(second_half, two[2 * p + 3:2 * p + 4], two[2 * p + 2:2 * p + 3])
+        edge_rows.append(jnp.where(upper, upper_unit, lower_unit))
+
+    for k, column in enumerate(slot_bins(count_ref, order_ref)):
+        bins = jnp.broadcast_to(column, (64, LANES))
+        rows = slice(k * 64, (k + 1) * 64)
+        for ref, line in ((hot_ref, rows_of), (edge_hot_ref, edge_rows)):
+            for n, wanted in enumerate(line):
+                ref[rows, n * LANES:(n + 1) * LANES] = jnp.where(
+                    bins == jnp.broadcast_to(wanted, (64, LANES)), 1.0, 0.0).astype(BF16)
 
     for i in range(STA):
         f_ref[i, STA * 8:(STA + 1) * 8, :] = zero
@@ -155,6 +176,15 @@
                 if s % 2 == 1:
                     d_ref[s // 2, own_rows, :] = jnp.where(
                         low_rows[:WIN], piece[rows], turned[(s + 1) * WIN:(s + 2) * WIN])
+            if b < 2:
+                for s in range(STA):
+                    for half in range(2):
+                        if b == 1 and s % 2 != half and s != STA - 1:
+                            continue
+                        unit = s if b == 0 else STA + s // 2
+                        base = (half * NG + g) * PITCH
+                        edge_t_ref[unit, pl.ds(base, WIN), :] = turned[s * WIN:(s + 1) * WIN]
+                        edge_s_ref[unit, pl.ds(base, WIN), :] = total[s * WIN:(s + 1) * WIN]
             before = [piece, turned_before]
             turned_before = turned
 
@@ -162,10 +192,6 @@
 
         def add(acc, key, w, v):
             acc[key] = v if w == 0 else acc[key] + v
-
-        def spread_of(k):
-            turned = pltpu.roll(k, 64, 1)
-            return jnp.where(low, k, turned), jnp.where(low, turned, k)
 
         for i in range(STA):
             k1, k1_own, k23 = {}, {}, {}
@@ -213,50 +239,47 @@
     out_ref[...] = (total[:, 0:128] + total[:, 128:256]) + (total[:, 256:384] + total[:, 384:512])
 
 
-def edge_kernel(own_ref, halo_ref, part_ref, hot_ref, out_ref, a_ref, t_ref, c_ref, x_ref):
-    sign = jnp.where(lane_iota((ROWS, LANES)) < 64, 1.0, -1.0).astype(F32)
+def edge_kernel(halo_ref, part_ref, hot_ref, t_ref, s_ref, out_ref, m_ref, d_ref, x_ref):
+    low = lane_iota((WIN, LANES)) < 64
+    low_rows = lane_iota((ROWS, LANES)) < 64
     zero = jnp.zeros((8, LANES), F32)
     for g in range(NG):
-        for slot, (ref, index) in enumerate(((own_ref, g), (own_ref, NG + g), (halo_ref, NG + g), (halo_ref, g))):
-            piece = ref[index, 0:ROWS, :].astype(F32)
+        for half in range(2):
+            piece = halo_ref[(1 - half) * NG + g, 0:ROWS, :].astype(F32)
+            turned = pltpu.roll(piece, 64, 1)
+            mixed = jnp.where(low_rows, piece - turned, piece + turned)
+            bases = [(0, (half * NG + g) * PITCH)]
+            if half == 0:
+                bases += [(1, g * PITCH), (1, (NG + g) * PITCH)]
             for s in range(STA):
-                rows = piece[s * WIN:(s + 1) * WIN]
-                if slot >= 2:
-                    base = ((slot - 2) * 4 + g) * PITCH
-                    c_ref[s, base:base + WIN, :] = rows
-                else:
-                    for half in range(2):
-                        base = (slot * 8 + half * 4 + g) * PITCH
-                        a_ref[s, base:base + WIN, :] = rows
-            if slot < 2:
-                turned = pltpu.roll(piece, 64, 1) * sign
-                for s in range(STA):
-                    for half in range(2):
-                        base = (slot * 8 + half * 4 + g) * PITCH
-                        t_ref[s, base:base + WIN, :] = turned[s * WIN:(s + 1) * WIN]
-
-    def per_station(i, carry):
-        for variant in range(2):
-            p, q = {}, {}
-            for w in range(WIN):
-                a = a_ref[i, pl.ds(variant * 8 * PITCH + w, 8, stride=PITCH), :]
-                t = t_ref[i, pl.ds(variant * 8 * PITCH + w, 8, stride=PITCH), :]
-                for j in range(STA):
-                    c = c_ref[j, pl.ds(w, 8, stride=PITCH), :]
-                    v = a * c
-                    p[j] = v if w == 0 else p[j] + v
-                    v = t * c
-                    q[j] = v if w == 0 else q[j] + v
-            values = [joined(p[j], q[j]) for j in range(STA)] + [zero]
-            for j in range(0, 8, 2):
-                pair = jnp.concatenate([values[j], values[j + 1]], axis=0).astype(BF16)
-                x_ref[i, (variant * 8 + j) * 8:(variant * 8 + j + 2) * 8, :] = pair
-        return carry
-
-    lax.fori_loop(0, STA, per_station, 0)
-    total = part_ref[...]
-    for i in range(STA):
-        total = total + jnp.dot(hot_ref[:, i * LANES:(i + 1) * LANES], x_ref[i], preferred_element_type=F32)
+                for kind, base in bases:
+                    m_ref[kind * STA + s, base:base + WIN, :] = mixed[s * WIN:(s + 1) * WIN]
+            for n in range(4):
+                s, t = 2 * n, min(2 * n + 1, STA - 1)
+                shared = jnp.where(low, piece[s * WIN:(s + 1) * WIN], turned[t * WIN:(t + 1) * WIN])
+                for kind, base in bases:
+                    d_ref[kind * 4 + n, base:base + WIN, :] = shared
+
+    x_ref[3 * LANES + 64:4 * LANES, :] = jnp.zeros((64, LANES), BF16)
+    for unit in range(STA + 4):
+        kind = 0 if unit < STA else 1
+        k1, k23 = {}, {}
+        for w in range(WIN):
+            rows = pl.ds(w, 8, stride=PITCH)
+            t = t_ref[unit, rows, :]
+            total = s_ref[unit, rows, :]
+            for j in range(STA):
+                v = t * m_ref[kind * STA + j, rows, :]
+                k23[j] = v if w == 0 else k23[j] + v
+            for n in range(4):
+                v = total * d_ref[kind * 4 + n, rows, :]
+                k1[n] = v if w == 0 else k1[n] + v
+        base = (unit if kind == 0 else unit + 1) * 64
+        for n in range(4):
+            lower, upper = spread_of(k1[n])
+            values = [lower - k23[2 * n], upper - k23[2 * n + 1] if n < 3 else zero]
+            x_ref[base + n * 16:base + (n + 1) * 16, :] = jnp.concatenate(values, axis=0).astype(BF16)
+    total = part_ref[...] + jnp.dot(hot_ref[...], x_ref[...], preferred_element_type=F32)
     for w, tile in enumerate(chunk_transpose([total[k * 64:(k + 1) * 64, :] for k in range(CAP)])):
         out_ref[pl.ds(w, 64, stride=4), :] = tile
 
@@ -278,28 +301,43 @@
 
 def on_device(spectra, pair_bins, owner_count, bin_order):
     vmem = pl.BlockSpec(memory_space=pltpu.VMEM)
-    packed = pl.pallas_call(
+    in_hbm = pl.BlockSpec(memory_space=pl.ANY)
+    packed, counts, order = pl.pallas_call(
         pack_kernel,
-        out_shape=pltpu.VMEM((32, MSG, LANES), BF16),
-        in_specs=[pl.BlockSpec(memory_space=pl.ANY)] * 2,
-        out_specs=vmem,
+        out_shape=(
+            pltpu.VMEM((32, MSG, LANES), BF16),
+            pltpu.VMEM((1, owner_count.shape[0]), jnp.int32),
+            pltpu.VMEM((1, bin_order.shape[0]), jnp.int32),
+        ),
+        in_specs=[in_hbm] * 4,
+        out_specs=(vmem,) * 3,
         scratch_shapes=[
             pltpu.VMEM((STA, WIN, 4096), BF16),
             pltpu.VMEM((ROUNDS, STA, STA), jnp.int32),
             pltpu.SemaphoreType.DMA((STA,)),
-            pltpu.SemaphoreType.DMA,
+            pltpu.SemaphoreType.DMA((3,)),
         ],
         name="pack",
-    )(jnp.transpose(spectra, (1, 0, 2)), jnp.transpose(pair_bins, (1, 0, 2)))
+    )(
+        jnp.transpose(spectra, (1, 0, 2)),
+        jnp.transpose(pair_bins, (1, 0, 2)),
+        owner_count.reshape(1, -1),
+        bin_order.reshape(1, -1),
+    )
     own = lax.all_to_all(packed, ("y", "c", "win"), 0, 0)
     count = lax.axis_size("z")
     halo = lax.ppermute(own[24:32], "z", [(i, (i + 1) % count) for i in range(count)])
-    own = in_vmem(own)
-    part, edge_hot = pl.pallas_call(
+    units = STA + 4
+    between = pl.pallas_call(
         cross_kernel,
-        out_shape=(pltpu.VMEM((256, LANES), F32), pltpu.VMEM((256, STA * LANES), BF16)),
+        out_shape=(
+            pltpu.VMEM((256, LANES), F32),
+            pltpu.VMEM((256, 6 * LANES), BF16),
+            pltpu.VMEM((units, 8 * PITCH, LANES), F32),
+            pltpu.VMEM((units, 8 * PITCH, LANES), F32),
+        ),
         in_specs=[vmem] * 3,
-        out_specs=(vmem, vmem),
+        out_specs=(vmem,) * 4,
         scratch_shapes=[
             pltpu.VMEM((STA, 144, LANES), F32),
             pltpu.VMEM((STA, 144, LANES), F32),
@@ -310,22 +348,22 @@
             pltpu.VMEM((STA * KI, NG * LANES), BF16),
             pltpu.VMEM((256, STA * KI), BF16),
         ],
+        compiler_params=SMALL,
         name="cross",
-    )(own, in_vmem(owner_count.reshape(1, -1)), in_vmem(bin_order.reshape(1, -1)))
-    halo = in_vmem(halo)
+    )(in_vmem(own), in_vmem(counts), in_vmem(order))
     send = pl.pallas_call(
         edge_kernel,
         out_shape=pltpu.VMEM((256, LANES), F32),
-        in_specs=[vmem] * 4,
+        in_specs=[vmem] * 5,
         out_specs=vmem,
         scratch_shapes=[
-            pltpu.VMEM((STA, 16 * PITCH, LANES), F32),
-            pltpu.VMEM((STA, 16 * PITCH, LANES), F32),
-            pltpu.VMEM((STA, 8 * PITCH, LANES), F32),
-            pltpu.VMEM((STA, LANES, LANES), BF16),
+            pltpu.VMEM((2 * STA, 8 * PITCH, LANES), F32),
+            pltpu.VMEM((8, 8 * PITCH, LANES), F32),
+            pltpu.VMEM((6 * LANES, LANES), BF16),
         ],
+        compiler_params=SMALL,
         name="edge",
-    )(own, halo, in_vmem(part), in_vmem(edge_hot))
+    )(in_vmem(halo), *(in_vmem(v) for v in between))
     got = lax.all_to_all(send.reshape(256, 1, LANES), ("z", "y", "c", "win"), 0, 0)
     got = in_vmem(got.reshape(8, 32, LANES))
     return pl.pallas_call(
@@ -334,6 +372,7 @@
         in_specs=[vmem],
         out_specs=vmem,
         scratch_shapes=[pltpu.VMEM((32, LANES), F32)],
+        compiler_params=SMALL,
         name="finish",
     )(got)
 

time: 63 us -> 61.9 us (0.983)
  Pallas kernels: 11.6 us -> 10.6 us
  local copies, waits for them, and re-layouts: 0.69 us -> 0.02 us
    pallas_call x1, Pallas kernels: 2.23 us -> 1.24 us  [on_device(): pl.pallas_call(edge_kernel, out_shape=pltpu.VMEM((256, LANES), F32), in_s...]
    unnamed x4 -> x0, local copies, waits for them, and re-layouts: 0.67 us -> none
where the time goes in v4:
time: 61.9 us; the launch traced here: 61.8 us
  blocking collectives  46.4 us (75%)
  Pallas kernels  10.6 us (17%)
  waiting for transfers between devices  2.97 us (5%)
  starting transfers between devices  1.71 us (3%)
    all_to_all x1, blocking collectives, on_device(): own = lax.all_to_all(packed, ('y', 'c', 'win'), 0, 0)  23.8 us
    all_to_all x1, blocking collectives, on_device(): lax.all_to_all(send.reshape(256, 1, LANES), ('z', 'y', 'c', 'win'), 0, 0)  22.6 us
    pallas_call x1, Pallas kernels, on_device(): pl.pallas_call(cross_kernel, out_shape=(pltpu.VMEM((256, LANES), F32), pl...  6.12 us
    ppermute x1, waiting for transfers between devices, on_device(): lax.ppermute(own[24:32], 'z', [(i, (i + 1) % count) for i in range(count)])  2.97 us
    pallas_call x1, Pallas kernels, on_device(): pl.pallas_call(pack_kernel, out_shape=(pltpu.VMEM((32, MSG, LANES), BF16)...  2.5 us
    ppermute x1, starting transfers between devices, on_device(): lax.ppermute(own[24:32], 'z', [(i, (i + 1) % count) for i in range(count)])  1.71 us
  transfers between devices with their start and end apart: 1, of which 1 were waited for; matrix products, arithmetic and copies ran while one was open for 0% of the time, Pallas kernels for 10%

profile of v4, /device:TPU:1, one launch (start us, length us, event | category | flops | bytes accessed | tf_op | source)
XLA Modules:
  0.0 61.8 jit_solution(7144010730620473405)
XLA Ops:
  0.0 2.5 %pack.1 = (bf16[32,120,128]{2,1,0:T(8,128)(2,1)S(1)}, s32[1,64]{1,0:T(1,128)S(1)}, s32[1,128]{1,0:T(1,128)S(1)}) custom-call(bf16[7,16,4096]{2,1,0:T(8,128)(2,1)} %bitcast.10, s32[3,7,7]{2,1,0:T(8,128)} %bitcast.11, s32[1,64]{1,0:T(1,128)} %bitcast.12, s32[1,128]{1,0:T(1,128)} %bitcast.13), custom_call_target="tpu_custom_call" | custom-call | tf_op jit(solution)/shard_map/pack/pallas_call | solution.py:305
  2.5 23.8 %all_to_all.10.own_ref = bf16[32,120,128]{2,1,0:T(8,128)(2,1)S(1)} all-to-all(bf16[32,120,128]{2,1,0:T(8,128)(2,1)S(1)} %get-tuple-element.12), channel_id=1, replica_groups=mesh['z'=8,'y'=4,'c'=2,'win'=4] {'y','c','win'}, dimensions={0} | all-to-all | bytes 1966080 | tf_op jit(solution)/shard_map/all_to_all | solution.py:327
  26.4 1.7 %collective-permute-start = (bf16[8,120,128]{2,1,0:T(8,128)(2,1)S(1)}, bf16[8,120,128]{2,1,0:T(8,128)(2,1)S(1)}, u32[]{:S(2)}, u32[]{:S(2)}) collective-permute-start(bf16[8,120,128]{2,1,0:T(8,128)(2,1)S(1)} %slice.4), channel_id=1, source_target_pairs={{0,32},{32,64},{64,96},{96,128},{128,160},{160,192},{192,224},{224... | collective-permute-start | bytes 737288 | tf_op jit(solution)/shard_map/ppermute | solution.py:329
  28.1 6.1 %cross.1 = (f32[256,128]{1,0:T(8,128)S(1)}, bf16[256,768]{1,0:T(8,128)(2,1)S(1)}, f32[11,136,128]{2,1,0:T(8,128)S(1)}, f32[11,136,128]{2,1,0:T(8,128)S(1)}) custom-call(bf16[32,120,128]{2,1,0:T(8,128)(2,1)S(1)} %all_to_all.10.own_ref, s32[1,64]{1,0:T(1,128)S(1)} %get-tuple-element.13.count_ref, s32[1,128]{1,0:T(1,128)S(1)} %get-tuple-element.14.order_ref), custom_call_target="tpu_custom_call" | custom-call | tf_op jit(solution)/shard_map/cross/pallas_call | solution.py:331
  34.2 3.0 %collective-permute-done.halo_ref = bf16[8,120,128]{2,1,0:T(8,128)(2,1)S(1)} collective-permute-done((bf16[8,120,128]{2,1,0:T(8,128)(2,1)S(1)}, bf16[8,120,128]{2,1,0:T(8,128)(2,1)S(1)}, u32[]{:S(2)}, u32[]{:S(2)}) %collective-permute-start) | collective-permute-done | bytes 245792 | tf_op jit(solution)/shard_map/ppermute | solution.py:329
  37.2 1.2 %edge.1 = f32[256,128]{1,0:T(8,128)S(1)} custom-call(bf16[8,120,128]{2,1,0:T(8,128)(2,1)S(1)} %collective-permute-done.halo_ref, f32[256,128]{1,0:T(8,128)S(1)} %get-tuple-element.15.part_ref, bf16[256,768]{1,0:T(8,128)(2,1)S(1)} %get-tuple-element.16.hot_ref, f32[11,136,128]{2,1,0:T(8,128)S(1)} %get-tuple-element.17.t_ref, ...), custom_call_target="tpu_custom_call" | custom-call | tf_op jit(solution)/shard_map/edge/pallas_call | solution.py:354
  38.4 22.6 %all_to_all.11 = f32[256,1,128]{2,1,0:T(1,128)S(1)} all-to-all(f32[256,1,128]{2,1,0:T(1,128)S(1)} %bitcast.8), channel_id=1, replica_groups=mesh['z'=8,'y'=4,'c'=2,'win'=4] {'z','y','c','win'}, dimensions={0} | all-to-all | bytes 262144 | tf_op jit(solution)/shard_map/all_to_all | solution.py:367
  61.0 0.8 %finish.1 = f32[4,1024]{1,0:T(4,128)} custom-call(f32[8,32,128]{2,1,0:T(8,128)S(1)} %bitcast.9), custom_call_target="tpu_custom_call" | custom-call | tf_op jit(solution)/shard_map/finish/pallas_call | solution.py:369
  (1 shorter events, 0.0 us)
Async XLA Ops:
  26.4 10.8 %collective-permute-start = (bf16[8,120,128]{2,1,0:T(8,128)(2,1)S(1)}, bf16[8,120,128]{2,1,0:T(8,128)(2,1)S(1)}, u32[]{:S(2)}, u32[]{:S(2)}) collective-permute-start(bf16[8,120,128]{2,1,0:T(8,128)(2,1)S(1)} %slice.4), channel_id=1, source_target_pairs={{0,32},{32,64},{64,96},{96,128},{128,160},{160,192},{192,224},{224... | collective-permute-start | bytes 737288 | tf_op jit(solution)/shard_map/ppermute | solution.py:329

commit v5 on v4

--- a/solution.py
+++ b/solution.py
@@ -32,16 +32,13 @@
     even = (lane % 64) < CHUNK
     axis = tiles[0].ndim - 1
 
-    def half(a, b):
-        return jnp.where(low, a, pltpu.roll(b, 64, axis)), jnp.where(low, pltpu.roll(a, 64, axis), b)
-
-    def quarter(a, b):
-        return jnp.where(even, a, pltpu.roll(b, CHUNK, axis)), jnp.where(even, pltpu.roll(a, LANES - CHUNK, axis), b)
-
-    u0, u2 = half(tiles[0], tiles[2])
-    u1, u3 = half(tiles[1], tiles[3])
-    v0, v1 = quarter(u0, u1)
-    v2, v3 = quarter(u2, u3)
+    def diagonals(a, b, c, d):
+        ab, cd = jnp.where(even, a, b), jnp.where(even, c, d)
+        bc, da = jnp.where(even, b, c), jnp.where(even, d, a)
+        return jnp.where(low, ab, cd), jnp.where(low, bc, da), jnp.where(low, cd, ab), jnp.where(low, da, bc)
+
+    g0, g1, g2, g3 = diagonals(*tiles)
+    v0, v3, v2, v1 = diagonals(g0, *(pltpu.roll(g, k * CHUNK, axis) for k, g in ((1, g1), (2, g2), (3, g3))))
     return v0, v1, v2, v3
 
 
@@ -326,7 +323,7 @@
     )
     own = lax.all_to_all(packed, ("y", "c", "win"), 0, 0)
     count = lax.axis_size("z")
-    halo = lax.ppermute(own[24:32], "z", [(i, (i + 1) % count) for i in range(count)])
+    halo = lax.ppermute(own[24:32, :ROWS], "z", [(i, (i + 1) % count) for i in range(count)])
     units = STA + 4
     between = pl.pallas_call(
         cross_kernel,

time: 61.9 us -> 60.9 us (0.984)
  Pallas kernels: 10.6 us -> 9.92 us
where the time goes in v5:
time: 60.9 us; the launch traced here: 60.7 us
  blocking collectives  46.4 us (76%)
  Pallas kernels  9.92 us (16%)
  waiting for transfers between devices  2.62 us (4%)
  starting transfers between devices  1.71 us (3%)
    all_to_all x1, blocking collectives, on_device(): own = lax.all_to_all(packed, ('y', 'c', 'win'), 0, 0)  23.8 us
    all_to_all x1, blocking collectives, on_device(): lax.all_to_all(send.reshape(256, 1, LANES), ('z', 'y', 'c', 'win'), 0, 0)  22.6 us
    pallas_call x1, Pallas kernels, on_device(): pl.pallas_call(cross_kernel, out_shape=(pltpu.VMEM((256, LANES), F32), pl...  6.12 us
    ppermute x1, waiting for transfers between devices, on_device(): lax.ppermute(own[24:32, :ROWS], 'z', [(i, (i + 1) % count) for i in range...  2.62 us
    pallas_call x1, Pallas kernels, on_device(): pl.pallas_call(pack_kernel, out_shape=(pltpu.VMEM((32, MSG, LANES), BF16)...  1.95 us
    ppermute x1, starting transfers between devices, on_device(): lax.ppermute(own[24:32, :ROWS], 'z', [(i, (i + 1) % count) for i in range...  1.71 us
  transfers between devices with their start and end apart: 1, of which 1 were waited for; matrix products, arithmetic and copies ran while one was open for 0% of the time, Pallas kernels for 10%

profile of v5, /device:TPU:1, one launch (start us, length us, event | category | flops | bytes accessed | tf_op | source)
XLA Modules:
  0.0 60.7 jit_solution(3666244020241304836)
XLA Ops:
  0.0 2.0 %pack.1 = (bf16[32,120,128]{2,1,0:T(8,128)(2,1)S(1)}, s32[1,64]{1,0:T(1,128)S(1)}, s32[1,128]{1,0:T(1,128)S(1)}) custom-call(bf16[7,16,4096]{2,1,0:T(8,128)(2,1)} %bitcast.10, s32[3,7,7]{2,1,0:T(8,128)} %bitcast.11, s32[1,64]{1,0:T(1,128)} %bitcast.12, s32[1,128]{1,0:T(1,128)} %bitcast.13), custom_call_target="tpu_custom_call" | custom-call | tf_op jit(solution)/shard_map/pack/pallas_call | solution.py:302
  2.0 23.8 %all_to_all.10.own_ref = bf16[32,120,128]{2,1,0:T(8,128)(2,1)S(1)} all-to-all(bf16[32,120,128]{2,1,0:T(8,128)(2,1)S(1)} %get-tuple-element.12), channel_id=1, replica_groups=mesh['z'=8,'y'=4,'c'=2,'win'=4] {'y','c','win'}, dimensions={0} | all-to-all | bytes 1966080 | tf_op jit(solution)/shard_map/all_to_all | solution.py:324
  25.8 1.7 %collective-permute-start = (bf16[8,112,128]{2,1,0:T(8,128)(2,1)S(1)}, bf16[8,112,128]{2,1,0:T(8,128)(2,1)S(1)}, u32[]{:S(2)}, u32[]{:S(2)}) collective-permute-start(bf16[8,112,128]{2,1,0:T(8,128)(2,1)S(1)} %slice.4), channel_id=1, source_target_pairs={{0,32},{32,64},{64,96},{96,128},{128,160},{160,192},{192,224},{224... | collective-permute-start | bytes 688136 | tf_op jit(solution)/shard_map/ppermute | solution.py:326
  27.5 6.1 %cross.1 = (f32[256,128]{1,0:T(8,128)S(1)}, bf16[256,768]{1,0:T(8,128)(2,1)S(1)}, f32[11,136,128]{2,1,0:T(8,128)S(1)}, f32[11,136,128]{2,1,0:T(8,128)S(1)}) custom-call(bf16[32,120,128]{2,1,0:T(8,128)(2,1)S(1)} %all_to_all.10.own_ref, s32[1,64]{1,0:T(1,128)S(1)} %get-tuple-element.13.count_ref, s32[1,128]{1,0:T(1,128)S(1)} %get-tuple-element.14.order_ref), custom_call_target="tpu_custom_call" | custom-call | tf_op jit(solution)/shard_map/cross/pallas_call | solution.py:328
  33.6 2.6 %collective-permute-done.halo_ref = bf16[8,112,128]{2,1,0:T(8,128)(2,1)S(1)} collective-permute-done((bf16[8,112,128]{2,1,0:T(8,128)(2,1)S(1)}, bf16[8,112,128]{2,1,0:T(8,128)(2,1)S(1)}, u32[]{:S(2)}, u32[]{:S(2)}) %collective-permute-start) | collective-permute-done | bytes 229408 | tf_op jit(solution)/shard_map/ppermute | solution.py:326
  36.3 1.1 %edge.1 = f32[256,128]{1,0:T(8,128)S(1)} custom-call(bf16[8,112,128]{2,1,0:T(8,128)(2,1)S(1)} %collective-permute-done.halo_ref, f32[256,128]{1,0:T(8,128)S(1)} %get-tuple-element.15.part_ref, bf16[256,768]{1,0:T(8,128)(2,1)S(1)} %get-tuple-element.16.hot_ref, f32[11,136,128]{2,1,0:T(8,128)S(1)} %get-tuple-element.17.t_ref, ...), custom_call_target="tpu_custom_call" | custom-call | tf_op jit(solution)/shard_map/edge/pallas_call | solution.py:351
  37.4 22.6 %all_to_all.11 = f32[256,1,128]{2,1,0:T(1,128)S(1)} all-to-all(f32[256,1,128]{2,1,0:T(1,128)S(1)} %bitcast.8), channel_id=1, replica_groups=mesh['z'=8,'y'=4,'c'=2,'win'=4] {'z','y','c','win'}, dimensions={0} | all-to-all | bytes 262144 | tf_op jit(solution)/shard_map/all_to_all | solution.py:364
  60.0 0.7 %finish.1 = f32[4,1024]{1,0:T(4,128)} custom-call(f32[8,32,128]{2,1,0:T(8,128)S(1)} %bitcast.9), custom_call_target="tpu_custom_call" | custom-call | tf_op jit(solution)/shard_map/finish/pallas_call | solution.py:366
  (1 shorter events, 0.0 us)
Async XLA Ops:
  25.8 10.5 %collective-permute-start = (bf16[8,112,128]{2,1,0:T(8,128)(2,1)S(1)}, bf16[8,112,128]{2,1,0:T(8,128)(2,1)S(1)}, u32[]{:S(2)}, u32[]{:S(2)}) collective-permute-start(bf16[8,112,128]{2,1,0:T(8,128)(2,1)S(1)} %slice.4), channel_id=1, source_target_pairs={{0,32},{32,64},{64,96},{96,128},{128,160},{160,192},{192,224},{224... | collective-permute-start | bytes 688136 | tf_op jit(solution)/shard_map/ppermute | solution.py:326

commit v6 on v5

--- a/solution.py
+++ b/solution.py
@@ -105,8 +105,29 @@
     return jnp.where(low, k, turned), jnp.where(low, turned, k)
 
 
-def cross_kernel(own_ref, count_ref, order_ref, out_ref, edge_hot_ref, edge_t_ref, edge_s_ref,
-                 t_ref, s_ref, m_ref, e_ref, d_ref, f_ref, x_ref, hot_ref):
+def edge_labels(rows, first_round, second_round):
+    col = lane_iota((LANES, LANES))
+    row = lax.broadcasted_iota(jnp.int32, (LANES, LANES), 0)
+    half, station = (col % 8) // 4, (col % 64) // 8
+    out = []
+    for part, (ref, value) in enumerate(((first_round, rows[0]), (second_round, rows[1]))):
+        place = jnp.where((row == ref * 8 + station) & (half == part), 1.0, 0.0).astype(BF16)
+        out.append(jnp.dot(value, place, preferred_element_type=F32))
+    none = lax.broadcasted_iota(jnp.int32, (8, LANES), 0) == STA
+    return jnp.where(none, -2.0, out[0] + out[1])
+
+
+def partner_rows(m_ref, d_ref, piece, turned, mixed, there):
+    low = lane_iota((WIN, LANES)) < 64
+    for s in range(STA):
+        m_ref[s, there, :] = mixed[s * WIN:(s + 1) * WIN]
+    for n in range(4):
+        s, t = 2 * n, min(2 * n + 1, STA - 1)
+        d_ref[n, there, :] = jnp.where(low, piece[s * WIN:(s + 1) * WIN], turned[t * WIN:(t + 1) * WIN])
+
+
+def cross_kernel(own_ref, count_ref, order_ref, out_ref, edge_hot_ref, edge_t_ref, edge_s_ref, edge_m_ref, edge_d_ref,
+                 bins_ref, t_ref, s_ref, m_ref, e_ref, d_ref, f_ref, x_ref, hot_ref):
     lane = lane_iota((8, LANES))
     low = lane < 64
     zero = jnp.zeros((8, LANES), F32)
@@ -122,27 +143,14 @@
     labels = jnp.where(lane_q // 64 > qmod, -2.0, labels)
     rows_of = [labels[i:i + 1, h * LANES:(h + 1) * LANES] for i in range(STA) for h in range(2)]
 
-    col = lane_iota((LANES, LANES))
-    row = lax.broadcasted_iota(jnp.int32, (LANES, LANES), 0)
-    half, station = (col % 8) // 4, (col % 64) // 8
-    first = jnp.where(row == (1 + half) * 8 + station, 1.0, 0.0).astype(BF16)
-    second = jnp.where(row == 2 * 8 + station, 1.0, 0.0).astype(BF16)
-    one = jnp.dot(own_ref[0, ROWS:MSG, :], first, preferred_element_type=F32)
-    two = jnp.dot(own_ref[NG, ROWS:MSG, :], second, preferred_element_type=F32)
-    none = lax.broadcasted_iota(jnp.int32, (8, LANES), 0) == STA
-    one = jnp.where(none, -2.0, one)
-    two = jnp.where(none, -2.0, two)
-    lane_1 = lane_iota((1, LANES))
-    upper, second_half = lane_1 >= 64, lane_1 % 8 >= 4
+    one = edge_labels((own_ref[0, ROWS:MSG, :], own_ref[NG, ROWS:MSG, :]), 1, 2)
+    upper = lane_iota((1, LANES)) >= 64
     edge_rows = [jnp.where(upper, one[2 * p + 1:2 * p + 2], one[2 * p:2 * p + 1]) for p in range(4)]
-    for p in (0, 2):
-        lower_unit = jnp.where(second_half, two[2 * p + 1:2 * p + 2], two[2 * p:2 * p + 1])
-        upper_unit = jnp.where(second_half, two[2 * p + 3:2 * p + 4], two[2 * p + 2:2 * p + 3])
-        edge_rows.append(jnp.where(upper, upper_unit, lower_unit))
 
     for k, column in enumerate(slot_bins(count_ref, order_ref)):
         bins = jnp.broadcast_to(column, (64, LANES))
         rows = slice(k * 64, (k + 1) * 64)
+        bins_ref[rows, :] = bins
         for ref, line in ((hot_ref, rows_of), (edge_hot_ref, edge_rows)):
             for n, wanted in enumerate(line):
                 ref[rows, n * LANES:(n + 1) * LANES] = jnp.where(
@@ -175,13 +183,12 @@
                         low_rows[:WIN], piece[rows], turned[(s + 1) * WIN:(s + 2) * WIN])
             if b < 2:
                 for s in range(STA):
-                    for half in range(2):
-                        if b == 1 and s % 2 != half and s != STA - 1:
-                            continue
-                        unit = s if b == 0 else STA + s // 2
-                        base = (half * NG + g) * PITCH
-                        edge_t_ref[unit, pl.ds(base, WIN), :] = turned[s * WIN:(s + 1) * WIN]
-                        edge_s_ref[unit, pl.ds(base, WIN), :] = total[s * WIN:(s + 1) * WIN]
+                    there = pl.ds((b * NG + g) * PITCH, WIN)
+                    edge_t_ref[s, there, :] = turned[s * WIN:(s + 1) * WIN]
+                    edge_s_ref[s, there, :] = total[s * WIN:(s + 1) * WIN]
+            if b == PLANE - 2:
+                for half in range(2):
+                    partner_rows(edge_m_ref, edge_d_ref, piece, turned, mixed, pl.ds((half * NG + g) * PITCH, WIN))
             before = [piece, turned_before]
             turned_before = turned
 
@@ -236,47 +243,57 @@
     out_ref[...] = (total[:, 0:128] + total[:, 128:256]) + (total[:, 256:384] + total[:, 384:512])
 
 
-def edge_kernel(halo_ref, part_ref, hot_ref, t_ref, s_ref, out_ref, m_ref, d_ref, x_ref):
-    low = lane_iota((WIN, LANES)) < 64
+def edge_kernel(after_ref, before_ref, part_ref, hot_ref, t_ref, s_ref, own_m_ref, own_d_ref, bins_ref, out_ref,
+                m_ref, d_ref, after_t_ref, after_s_ref, x_ref, after_hot_ref):
     low_rows = lane_iota((ROWS, LANES)) < 64
     zero = jnp.zeros((8, LANES), F32)
     for g in range(NG):
+        piece = before_ref[g].astype(F32)
+        turned = pltpu.roll(piece, 64, 1)
+        mixed = jnp.where(low_rows, piece - turned, piece + turned)
         for half in range(2):
-            piece = halo_ref[(1 - half) * NG + g, 0:ROWS, :].astype(F32)
-            turned = pltpu.roll(piece, 64, 1)
-            mixed = jnp.where(low_rows, piece - turned, piece + turned)
-            bases = [(0, (half * NG + g) * PITCH)]
-            if half == 0:
-                bases += [(1, g * PITCH), (1, (NG + g) * PITCH)]
-            for s in range(STA):
-                for kind, base in bases:
-                    m_ref[kind * STA + s, base:base + WIN, :] = mixed[s * WIN:(s + 1) * WIN]
-            for n in range(4):
-                s, t = 2 * n, min(2 * n + 1, STA - 1)
-                shared = jnp.where(low, piece[s * WIN:(s + 1) * WIN], turned[t * WIN:(t + 1) * WIN])
-                for kind, base in bases:
-                    d_ref[kind * 4 + n, base:base + WIN, :] = shared
+            base = (half * NG + g) * PITCH
+            partner_rows(m_ref, d_ref, piece, turned, mixed, slice(base, base + WIN))
+        piece = after_ref[g, 0:ROWS, :].astype(F32)
+        turned = pltpu.roll(piece, 64, 1)
+        total = piece + turned
+        for n in range(8):
+            s, base = min(n, STA - 1), ((n % 2) * NG + g) * PITCH
+            after_t_ref[n // 2, base:base + WIN, :] = turned[s * WIN:(s + 1) * WIN]
+            after_s_ref[n // 2, base:base + WIN, :] = total[s * WIN:(s + 1) * WIN]
+
+    two = edge_labels((after_ref[0, ROWS:MSG, :],) * 2, 2, 2)
+    lane_1 = lane_iota((1, LANES))
+    upper, second_half = lane_1 >= 64, lane_1 % 8 >= 4
+    for p in (0, 2):
+        lower_unit = jnp.where(second_half, two[2 * p + 1:2 * p + 2], two[2 * p:2 * p + 1])
+        upper_unit = jnp.where(second_half, two[2 * p + 3:2 * p + 4], two[2 * p + 2:2 * p + 3])
+        wanted = jnp.broadcast_to(jnp.where(upper, upper_unit, lower_unit), (256, LANES))
+        after_hot_ref[:, p * 64:p * 64 + LANES] = jnp.where(bins_ref[...] == wanted, 1.0, 0.0).astype(BF16)
 
     x_ref[3 * LANES + 64:4 * LANES, :] = jnp.zeros((64, LANES), BF16)
     for unit in range(STA + 4):
-        kind = 0 if unit < STA else 1
+        here = unit < STA
+        own_t, own_s, place = (t_ref, s_ref, unit) if here else (after_t_ref, after_s_ref, unit - STA)
+        other_m, other_d = (m_ref, d_ref) if here else (own_m_ref, own_d_ref)
         k1, k23 = {}, {}
         for w in range(WIN):
             rows = pl.ds(w, 8, stride=PITCH)
-            t = t_ref[unit, rows, :]
-            total = s_ref[unit, rows, :]
+            t = own_t[place, rows, :]
+            total = own_s[place, rows, :]
             for j in range(STA):
-                v = t * m_ref[kind * STA + j, rows, :]
+                v = t * other_m[j, rows, :]
                 k23[j] = v if w == 0 else k23[j] + v
             for n in range(4):
-                v = total * d_ref[kind * 4 + n, rows, :]
+                v = total * other_d[n, rows, :]
                 k1[n] = v if w == 0 else k1[n] + v
-        base = (unit if kind == 0 else unit + 1) * 64
+        base = (unit if here else unit + 1) * 64
         for n in range(4):
             lower, upper = spread_of(k1[n])
             values = [lower - k23[2 * n], upper - k23[2 * n + 1] if n < 3 else zero]
             x_ref[base + n * 16:base + (n + 1) * 16, :] = jnp.concatenate(values, axis=0).astype(BF16)
-    total = part_ref[...] + jnp.dot(hot_ref[...], x_ref[...], preferred_element_type=F32)
+    total = part_ref[...] + jnp.dot(hot_ref[...], x_ref[0:4 * LANES, :], preferred_element_type=F32)
+    total = total + jnp.dot(after_hot_ref[...], x_ref[4 * LANES:, :], preferred_element_type=F32)
     for w, tile in enumerate(chunk_transpose([total[k * 64:(k + 1) * 64, :] for k in range(CAP)])):
         out_ref[pl.ds(w, 64, stride=4), :] = tile
 
@@ -323,18 +340,23 @@
     )
     own = lax.all_to_all(packed, ("y", "c", "win"), 0, 0)
     count = lax.axis_size("z")
-    halo = lax.ppermute(own[24:32, :ROWS], "z", [(i, (i + 1) % count) for i in range(count)])
-    units = STA + 4
+    before = lax.ppermute(own[28:32, :ROWS], "z", [(i, (i + 1) % count) for i in range(count)])
+    after = lax.ppermute(own[0:4], "z", [((i + 1) % count, i) for i in range(count)])
+    operand = pltpu.VMEM((STA, 8 * PITCH, LANES), F32)
+    shared = pltpu.VMEM((4, 8 * PITCH, LANES), F32)
     between = pl.pallas_call(
         cross_kernel,
         out_shape=(
             pltpu.VMEM((256, LANES), F32),
-            pltpu.VMEM((256, 6 * LANES), BF16),
-            pltpu.VMEM((units, 8 * PITCH, LANES), F32),
-            pltpu.VMEM((units, 8 * PITCH, LANES), F32),
+            pltpu.VMEM((256, 4 * LANES), BF16),
+            operand,
+            operand,
+            operand,
+            shared,
+            pltpu.VMEM((256, LANES), F32),
         ),
         in_specs=[vmem] * 3,
-        out_specs=(vmem,) * 4,
+        out_specs=(vmem,) * 7,
         scratch_shapes=[
             pltpu.VMEM((STA, 144, LANES), F32),
             pltpu.VMEM((STA, 144, LANES), F32),
@@ -351,16 +373,19 @@
     send = pl.pallas_call(
         edge_kernel,
         out_shape=pltpu.VMEM((256, LANES), F32),
-        in_specs=[vmem] * 5,
+        in_specs=[vmem] * 9,
         out_specs=vmem,
         scratch_shapes=[
-            pltpu.VMEM((2 * STA, 8 * PITCH, LANES), F32),
-            pltpu.VMEM((8, 8 * PITCH, LANES), F32),
+            operand,
+            shared,
+            shared,
+            shared,
             pltpu.VMEM((6 * LANES, LANES), BF16),
+            pltpu.VMEM((256, 2 * LANES), BF16),
         ],
         compiler_params=SMALL,
         name="edge",
-    )(in_vmem(halo), *(in_vmem(v) for v in between))
+    )(in_vmem(after), in_vmem(before), *(in_vmem(v) for v in between))
     got = lax.all_to_all(send.reshape(256, 1, LANES), ("z", "y", "c", "win"), 0, 0)
     got = in_vmem(got.reshape(8, 32, LANES))
     return pl.pallas_call(

time: 60.9 us -> 60.9 us (level)
  starting transfers between devices: 1.71 us -> 5.74 us
  waiting for transfers between devices: 2.62 us -> 0.01 us
  blocking collectives: 46.4 us -> 45 us
    ppermute x1 -> x2, starting transfers between devices: 1.71 us -> 5.74 us  [the longest x1 5.65 us: on_device(): lax.ppermute(own[0:4], 'z', [((i + 1) % count, i) for i in range(count)])]
    ppermute x1 -> x2, waiting for transfers between devices: 2.62 us -> 0.01 us  [the longest x1 0.01 us: on_device(): lax.ppermute(own[28:32, :ROWS], 'z', [(i, (i + 1) % count) for i in range...]
    all_to_all x1, blocking collectives: 22.6 us -> 21.2 us  [on_device(): lax.all_to_all(send.reshape(256, 1, LANES), ('z', 'y', 'c', 'win'), 0, 0)]
  transfers between devices with their start and end apart: 1 -> 2, of which waited for: 1 -> 0; matrix products, arithmetic and copies ran while one was open for 0% -> 0% of each run, Pallas kernels for 10% -> 10%
where the time goes in v6:
time: 60.9 us; the launch traced here: 60.7 us
  blocking collectives  45 us (74%)
  Pallas kernels  9.88 us (16%)
  starting transfers between devices  5.74 us (9%)
    all_to_all x1, blocking collectives, on_device(): own = lax.all_to_all(packed, ('y', 'c', 'win'), 0, 0)  23.8 us
    all_to_all x1, blocking collectives, on_device(): lax.all_to_all(send.reshape(256, 1, LANES), ('z', 'y', 'c', 'win'), 0, 0)  21.2 us
    pallas_call x1, Pallas kernels, on_device(): pl.pallas_call(cross_kernel, out_shape=(pltpu.VMEM((256, LANES), F32), pl...  6.1 us
    ppermute x1, starting transfers between devices, on_device(): lax.ppermute(own[0:4], 'z', [((i + 1) % count, i) for i in range(count)])  5.65 us
    pallas_call x1, Pallas kernels, on_device(): pl.pallas_call(pack_kernel, out_shape=(pltpu.VMEM((32, MSG, LANES), BF16)...  1.95 us
  transfers between devices with their start and end apart: 2, of which 0 were waited for; matrix products, arithmetic and copies ran while one was open for 0% of the time, Pallas kernels for 10%

profile of v6, /device:TPU:1, one launch (start us, length us, event | category | flops | bytes accessed | tf_op | source)
XLA Modules:
  0.0 60.7 jit_solution(11862364910158437346)
XLA Ops:
  0.0 2.0 %pack.1 = (bf16[32,120,128]{2,1,0:T(8,128)(2,1)S(1)}, s32[1,64]{1,0:T(1,128)S(1)}, s32[1,128]{1,0:T(1,128)S(1)}) custom-call(bf16[7,16,4096]{2,1,0:T(8,128)(2,1)} %bitcast.10, s32[3,7,7]{2,1,0:T(8,128)} %bitcast.11, s32[1,64]{1,0:T(1,128)} %bitcast.12, s32[1,128]{1,0:T(1,128)} %bitcast.13), custom_call_target="tpu_custom_call" | custom-call | tf_op jit(solution)/shard_map/pack/pallas_call | solution.py:319
  2.0 23.8 %all_to_all.10.own_ref = bf16[32,120,128]{2,1,0:T(8,128)(2,1)S(1)} all-to-all(bf16[32,120,128]{2,1,0:T(8,128)(2,1)S(1)} %get-tuple-element.15), channel_id=1, replica_groups=mesh['z'=8,'y'=4,'c'=2,'win'=4] {'y','c','win'}, dimensions={0} | all-to-all | bytes 1966080 | tf_op jit(solution)/shard_map/all_to_all | solution.py:341
  25.8 5.7 %collective-permute-start = (bf16[4,120,128]{2,1,0:T(8,128)(2,1)S(1)}, bf16[4,120,128]{2,1,0:T(8,128)(2,1)S(1)}, u32[]{:S(2)}, u32[]{:S(2)}) collective-permute-start(bf16[4,120,128]{2,1,0:T(8,128)(2,1)S(1)} %slice.8), channel_id=1, source_target_pairs={{32,0},{64,32},{96,64},{128,96},{160,128},{192,160},{224,192},{0,2... | collective-permute-start | bytes 368648 | tf_op jit(solution)/shard_map/ppermute | solution.py:344
  31.5 0.1 collective-permute-start.1
  31.6 6.1 %cross.1 = (f32[256,128]{1,0:T(8,128)S(1)}, bf16[256,512]{1,0:T(8,128)(2,1)S(1)}, f32[7,136,128]{2,1,0:T(8,128)S(1)}, f32[7,136,128]{2,1,0:T(8,128)S(1)}, f32[7,...) custom-call(bf16[32,120,128]{2,1,0:T(8,128)(2,1)S(1)} %all_to_all.10.own_ref, ...), custom_call_target="tpu_custom_call" | custom-call | tf_op jit(solution)/shard_map/cross/pallas_call | solution.py:347
  37.7 0.0 collective-permute-done.1.before_ref
  37.7 0.0 collective-permute-done.after_ref
  37.7 1.1 %edge.1 = f32[256,128]{1,0:T(8,128)S(1)} custom-call(bf16[4,120,128]{2,1,0:T(8,128)(2,1)S(1)} %collective-permute-done.after_ref, bf16[4,112,128]{2,1,0:T(8,128)(2,1)S(1)} %collective-permute-done.1.before_ref, f32[256,128]{1,0:T(8,128)S(1)} %get-tuple-element.18.part_ref, bf16[256,512]{1,0:T(8,128)(2,1)S(1)} %get-tuple-element.19.hot_ref, ...), custom_call_target="tpu_custom_call" | custom-call | tf_op jit(solution)/shard_map/edge/pallas_call | solution.py:373
  38.8 21.2 %all_to_all.11 = f32[256,1,128]{2,1,0:T(1,128)S(1)} all-to-all(f32[256,1,128]{2,1,0:T(1,128)S(1)} %bitcast.8), channel_id=1, replica_groups=mesh['z'=8,'y'=4,'c'=2,'win'=4] {'z','y','c','win'}, dimensions={0} | all-to-all | bytes 262144 | tf_op jit(solution)/shard_map/all_to_all | solution.py:389
  60.0 0.7 %finish.1 = f32[4,1024]{1,0:T(4,128)} custom-call(f32[8,32,128]{2,1,0:T(8,128)S(1)} %bitcast.9), custom_call_target="tpu_custom_call" | custom-call | tf_op jit(solution)/shard_map/finish/pallas_call | solution.py:391
  (2 shorter events, 0.0 us)
Async XLA Ops:
  25.8 11.9 %collective-permute-start = (bf16[4,120,128]{2,1,0:T(8,128)(2,1)S(1)}, bf16[4,120,128]{2,1,0:T(8,128)(2,1)S(1)}, u32[]{:S(2)}, u32[]{:S(2)}) collective-permute-start(bf16[4,120,128]{2,1,0:T(8,128)(2,1)S(1)} %slice.8), channel_id=1, source_target_pairs={{32,0},{64,32},{96,64},{128,96},{160,128},{192,160},{224,192},{0,2... | collective-permute-start | bytes 368648 | tf_op jit(solution)/shard_map/ppermute | solution.py:344
  31.5 6.2 %collective-permute-start.1 = (bf16[4,112,128]{2,1,0:T(8,128)(2,1)S(1)}, bf16[4,112,128]{2,1,0:T(8,128)(2,1)S(1)}, u32[]{:S(2)}, u32[]{:S(2)}) collective-permute-start(bf16[4,112,128]{2,1,0:T(8,128)(2,1)S(1)} %slice.9), channel_id=1, source_target_pairs={{0,32},{32,64},{64,96},{96,128},{128,160},{160,192},{192,224},{224... | collective-permute-start | bytes 344072 | tf_op jit(solution)/shard_map/ppermute | solution.py:343

commit v7 on v6

--- a/solution.py
+++ b/solution.py
@@ -79,24 +79,18 @@
     order_copy.wait()
 
 
-def slot_bins(count_ref, order_ref):
+def positions(count_ref, order_ref):
     row = lax.broadcasted_iota(jnp.int32, (64, 64), 0)
     lane = lax.broadcasted_iota(jnp.int32, (64, 64), 1)
     counts = jnp.broadcast_to(count_ref[...].astype(F32), (64, 64))
     start = jnp.sum(jnp.where(lane < row, counts, 0.0), axis=1, keepdims=True)
     count = jnp.sum(jnp.where(lane == row, counts, 0.0), axis=1, keepdims=True)
     lane = lax.broadcasted_iota(jnp.int32, (64, LANES), 1).astype(F32)
-    order = jnp.broadcast_to(order_ref[...].astype(F32), (64, LANES))
-    out = []
-    for k in range(CAP):
-        chosen = jnp.sum(jnp.where(lane == start + float(k), order, 0.0), axis=1, keepdims=True)
-        out.append(jnp.where(count > float(k), chosen, -1.0))
-    return out
-
-
-def joined(p, q):
-    low = lane_iota(p.shape) < 64
-    return jnp.where(low, p, q) + pltpu.roll(jnp.where(low, q, p), 64, 1)
+    slots = [jnp.where((lane == start + float(k)) & (count > float(k)), 1.0, 0.0).astype(BF16) for k in range(CAP)]
+    row = lax.broadcasted_iota(jnp.int32, (LANES, LANES), 0)
+    lane = lax.broadcasted_iota(jnp.int32, (LANES, LANES), 1)
+    order = jnp.broadcast_to(order_ref[...].astype(F32), (LANES, LANES))
+    return jnp.sum(jnp.where(lane == row, order, 0.0), axis=1, keepdims=True), slots
 
 
 def spread_of(k):
@@ -127,7 +121,8 @@
 
 
 def cross_kernel(own_ref, count_ref, order_ref, out_ref, edge_hot_ref, edge_t_ref, edge_s_ref, edge_m_ref, edge_d_ref,
-                 bins_ref, t_ref, s_ref, m_ref, e_ref, d_ref, f_ref, x_ref, hot_ref):
+                 bins_ref, slot_ref, *scratch):
+    sets, x_ref, hot_ref = (scratch[0:6],), scratch[6], scratch[7]
     lane = lane_iota((8, LANES))
     low = lane < 64
     zero = jnp.zeros((8, LANES), F32)
@@ -141,27 +136,32 @@
         wide = jnp.dot(own_ref[b * NG, ROWS:MSG, :], spread, preferred_element_type=F32)
         labels = labels + jnp.where(qmod == b, wide, 0.0)
     labels = jnp.where(lane_q // 64 > qmod, -2.0, labels)
+    labels = labels.astype(BF16)
     rows_of = [labels[i:i + 1, h * LANES:(h + 1) * LANES] for i in range(STA) for h in range(2)]
 
     one = edge_labels((own_ref[0, ROWS:MSG, :], own_ref[NG, ROWS:MSG, :]), 1, 2)
     upper = lane_iota((1, LANES)) >= 64
     edge_rows = [jnp.where(upper, one[2 * p + 1:2 * p + 2], one[2 * p:2 * p + 1]) for p in range(4)]
 
-    for k, column in enumerate(slot_bins(count_ref, order_ref)):
-        bins = jnp.broadcast_to(column, (64, LANES))
-        rows = slice(k * 64, (k + 1) * 64)
-        bins_ref[rows, :] = bins
-        for ref, line in ((hot_ref, rows_of), (edge_hot_ref, edge_rows)):
-            for n, wanted in enumerate(line):
-                ref[rows, n * LANES:(n + 1) * LANES] = jnp.where(
-                    bins == jnp.broadcast_to(wanted, (64, LANES)), 1.0, 0.0).astype(BF16)
+    column, slots = positions(count_ref, order_ref)
+    for k in range(CAP):
+        slot_ref[k * 64:(k + 1) * 64, :] = slots[k]
+    bins = jnp.broadcast_to(column, (LANES, LANES)).astype(BF16)
+    bins_ref[...] = bins
+    one_bf16, zero_bf16 = jnp.ones((LANES, LANES), BF16), jnp.zeros((LANES, LANES), BF16)
+    for ref, line in ((hot_ref, rows_of), (edge_hot_ref, edge_rows)):
+        for n, wanted in enumerate(line):
+            ref[:, n * LANES:(n + 1) * LANES] = jnp.where(
+                bins == jnp.broadcast_to(wanted.astype(BF16), (LANES, LANES)), one_bf16, zero_bf16)
 
     for i in range(STA):
-        f_ref[i, STA * 8:(STA + 1) * 8, :] = zero
         x_ref[i * KI + ROUNDS * 64:(i + 1) * KI, :] = jnp.zeros((64, NG * LANES), BF16)
-        m_ref[i, 0:2 * PITCH, :] = jnp.zeros((2 * PITCH, LANES), F32)
-
-    def per_shard(g, carry):
+        for _, _, m_ref, _, _, f_ref in sets:
+            f_ref[i, STA * 8:(STA + 1) * 8, :] = zero
+            m_ref[i, 0:2 * PITCH, :] = jnp.zeros((2 * PITCH, LANES), F32)
+
+    def prepare(g, refs):
+        t_ref, s_ref, m_ref, e_ref, d_ref, _ = refs
         low_rows = lane_iota((ROWS, LANES)) < 64
         before = [jnp.zeros((ROWS, LANES), F32)] * 2
         turned_before = jnp.zeros((ROWS, LANES), F32)
@@ -192,31 +192,42 @@
             before = [piece, turned_before]
             turned_before = turned
 
+    def compute(g, refs):
+        t_ref, s_ref, m_ref, e_ref, d_ref, f_ref = refs
         lanes = pl.ds(pl.multiple_of(g * LANES, LANES), LANES)
 
         def add(acc, key, w, v):
             acc[key] = v if w == 0 else acc[key] + v
 
-        for i in range(STA):
-            k1, k1_own, k23 = {}, {}, {}
-            pairs = [n for n in range(3) if 2 * n + 2 > i]
+        for group in ((0, 1), (2, 3), (4, 5), (6,)):
+            k1, k23 = {}, {}
             for w in range(WIN):
                 rows = pl.ds(w, 8, stride=PITCH)
-                t = t_ref[i, rows, :]
-                total = s_ref[i, rows, :]
-                add(k23, (0, i), w, t * t)
-                for j in range(i + 1, STA):
-                    add(k23, (0, j), w, t * m_ref[j, pl.ds(2 * PITCH + w, 8, stride=PITCH), :])
-                for n in pairs:
-                    add(k1_own, n, w, total * d_ref[n, rows, :])
-            auto = k23[0, i]
-            f_ref[i, i * 8:(i + 1) * 8, :] = jnp.where(low, auto + pltpu.roll(auto, 64, 1), 0.0)
-            for n in pairs:
-                for j, k in zip((2 * n + 1, 2 * n + 2), spread_of(k1_own[n])):
+                t = {i: t_ref[i, rows, :] for i in group}
+                total = {i: s_ref[i, rows, :] for i in group}
+                for i in group:
+                    add(k23, (i, i), w, t[i] * t[i])
+                for j in range(group[0] + 1, STA):
+                    mixed = m_ref[j, pl.ds(2 * PITCH + w, 8, stride=PITCH), :]
+                    for i in group:
+                        if i < j:
+                            add(k23, (i, j), w, t[i] * mixed)
+                for n in range(group[0] // 2, 3 if group[0] < 6 else 0):
+                    shared = d_ref[n, rows, :]
+                    for i in group:
+                        if i < 2 * n + 2:
+                            add(k1, (i, n), w, total[i] * shared)
+            for i in group:
+                auto = k23[i, i]
+                f_ref[i, i * 8:(i + 1) * 8, :] = jnp.where(low, auto + pltpu.roll(auto, 64, 1), 0.0)
+            for (i, n), k in k1.items():
+                for j, part in zip((2 * n + 1, 2 * n + 2), spread_of(k)):
                     if j > i:
-                        value = k - k23[0, j]
+                        value = part - k23[i, j]
                         f_ref[i, j * 8:(j + 1) * 8, :] = value
                         f_ref[j, i * 8:(i + 1) * 8, :] = jnp.where(low, value, -value)
+        for i in range(STA):
+            k1, k23 = {}, {}
             for w in range(WIN):
                 rows = pl.ds(w, 8, stride=PITCH)
                 t = t_ref[i, rows, :]
@@ -236,6 +247,10 @@
                     x_ref[base:base + 16, lanes] = pair
         for i in range(STA):
             x_ref[i * KI:i * KI + 64, lanes] = f_ref[i].astype(BF16)
+
+    def per_shard(g, carry):
+        prepare(g, sets[0])
+        compute(g, sets[0])
         return carry
 
     lax.fori_loop(0, NG, per_shard, 0)
@@ -243,7 +258,7 @@
     out_ref[...] = (total[:, 0:128] + total[:, 128:256]) + (total[:, 256:384] + total[:, 384:512])
 
 
-def edge_kernel(after_ref, before_ref, part_ref, hot_ref, t_ref, s_ref, own_m_ref, own_d_ref, bins_ref, out_ref,
+def edge_kernel(after_ref, before_ref, part_ref, hot_ref, t_ref, s_ref, own_m_ref, own_d_ref, bins_ref, slot_ref, out_ref,
                 m_ref, d_ref, after_t_ref, after_s_ref, x_ref, after_hot_ref):
     low_rows = lane_iota((ROWS, LANES)) < 64
     zero = jnp.zeros((8, LANES), F32)
@@ -268,8 +283,9 @@
     for p in (0, 2):
         lower_unit = jnp.where(second_half, two[2 * p + 1:2 * p + 2], two[2 * p:2 * p + 1])
         upper_unit = jnp.where(second_half, two[2 * p + 3:2 * p + 4], two[2 * p + 2:2 * p + 3])
-        wanted = jnp.broadcast_to(jnp.where(upper, upper_unit, lower_unit), (256, LANES))
-        after_hot_ref[:, p * 64:p * 64 + LANES] = jnp.where(bins_ref[...] == wanted, 1.0, 0.0).astype(BF16)
+        wanted = jnp.broadcast_to(jnp.where(upper, upper_unit, lower_unit).astype(BF16), (LANES, LANES))
+        after_hot_ref[:, p * 64:p * 64 + LANES] = jnp.where(
+            bins_ref[...] == wanted, jnp.ones((LANES, LANES), BF16), jnp.zeros((LANES, LANES), BF16))
 
     x_ref[3 * LANES + 64:4 * LANES, :] = jnp.zeros((64, LANES), BF16)
     for unit in range(STA + 4):
@@ -294,6 +310,12 @@
             x_ref[base + n * 16:base + (n + 1) * 16, :] = jnp.concatenate(values, axis=0).astype(BF16)
     total = part_ref[...] + jnp.dot(hot_ref[...], x_ref[0:4 * LANES, :], preferred_element_type=F32)
     total = total + jnp.dot(after_hot_ref[...], x_ref[4 * LANES:, :], preferred_element_type=F32)
+    parts = []
+    for _ in range(3):
+        parts.append(total.astype(BF16))
+        total = total - parts[-1].astype(F32)
+    total = jnp.dot(slot_ref[...], jnp.concatenate(parts, axis=1), preferred_element_type=F32)
+    total = (total[:, 0:128] + total[:, 128:256]) + total[:, 256:384]
     for w, tile in enumerate(chunk_transpose([total[k * 64:(k + 1) * 64, :] for k in range(CAP)])):
         out_ref[pl.ds(w, 64, stride=4), :] = tile
 
@@ -347,25 +369,22 @@
     between = pl.pallas_call(
         cross_kernel,
         out_shape=(
-            pltpu.VMEM((256, LANES), F32),
-            pltpu.VMEM((256, 4 * LANES), BF16),
+            pltpu.VMEM((LANES, LANES), F32),
+            pltpu.VMEM((LANES, 4 * LANES), BF16),
             operand,
             operand,
             operand,
             shared,
-            pltpu.VMEM((256, LANES), F32),
+            pltpu.VMEM((LANES, LANES), BF16),
+            pltpu.VMEM((256, LANES), BF16),
         ),
         in_specs=[vmem] * 3,
-        out_specs=(vmem,) * 7,
+        out_specs=(vmem,) * 8,
         scratch_shapes=[
-            pltpu.VMEM((STA, 144, LANES), F32),
-            pltpu.VMEM((STA, 144, LANES), F32),
-            pltpu.VMEM((STA, 176, LANES), F32),
-            pltpu.VMEM((STA, 144, LANES), F32),
-            pltpu.VMEM((3, 144, LANES), F32),
-            pltpu.VMEM((STA, 64, LANES), F32),
+            *(pltpu.VMEM((count, rows, LANES), F32)
+              for count, rows in ((STA, 144), (STA, 144), (STA, 176), (STA, 144), (3, 144), (STA, 64))),
             pltpu.VMEM((STA * KI, NG * LANES), BF16),
-            pltpu.VMEM((256, STA * KI), BF16),
+            pltpu.VMEM((LANES, STA * KI), BF16),
         ],
         compiler_params=SMALL,
         name="cross",
@@ -373,7 +392,7 @@
     send = pl.pallas_call(
         edge_kernel,
         out_shape=pltpu.VMEM((256, LANES), F32),
-        in_specs=[vmem] * 9,
+        in_specs=[vmem] * 10,
         out_specs=vmem,
         scratch_shapes=[
             operand,
@@ -381,7 +400,7 @@
             shared,
             shared,
             pltpu.VMEM((6 * LANES, LANES), BF16),
-            pltpu.VMEM((256, 2 * LANES), BF16),
+            pltpu.VMEM((LANES, 2 * LANES), BF16),
         ],
         compiler_params=SMALL,
         name="edge",

time: 60.9 us -> 60.7 us (level)
  transfers between devices with their start and end apart: 2 -> 2, of which waited for: 0 -> 0; matrix products, arithmetic and copies ran while one was open for 0% -> 0% of each run, Pallas kernels for 10% -> 9%
where the time goes in v7:
time: 60.7 us; the launch traced here: 60.5 us
  blocking collectives  45 us (74%)
  Pallas kernels  9.71 us (16%)
  starting transfers between devices  5.74 us (9%)
    all_to_all x1, blocking collectives, on_device(): own = lax.all_to_all(packed, ('y', 'c', 'win'), 0, 0)  23.8 us
    all_to_all x1, blocking collectives, on_device(): lax.all_to_all(send.reshape(256, 1, LANES), ('z', 'y', 'c', 'win'), 0, 0)  21.2 us
    pallas_call x1, Pallas kernels, on_device(): pl.pallas_call(cross_kernel, out_shape=(pltpu.VMEM((LANES, LANES), F32),...  5.71 us
    ppermute x1, starting transfers between devices, on_device(): lax.ppermute(own[0:4], 'z', [((i + 1) % count, i) for i in range(count)])  5.65 us
    pallas_call x1, Pallas kernels, on_device(): pl.pallas_call(pack_kernel, out_shape=(pltpu.VMEM((32, MSG, LANES), BF16)...  1.95 us
    pallas_call x1, Pallas kernels, on_device(): pl.pallas_call(edge_kernel, out_shape=pltpu.VMEM((256, LANES), F32), in_s...  1.34 us
  transfers between devices with their start and end apart: 2, of which 0 were waited for; matrix products, arithmetic and copies ran while one was open for 0% of the time, Pallas kernels for 9%

profile of v7, /device:TPU:1, one launch (start us, length us, event | category | flops | bytes accessed | tf_op | source)
XLA Modules:
  0.0 60.5 jit_solution(16437924740913286499)
XLA Ops:
  0.0 2.0 %pack.1 = (bf16[32,120,128]{2,1,0:T(8,128)(2,1)S(1)}, s32[1,64]{1,0:T(1,128)S(1)}, s32[1,128]{1,0:T(1,128)S(1)}) custom-call(bf16[7,16,4096]{2,1,0:T(8,128)(2,1)} %bitcast.10, s32[3,7,7]{2,1,0:T(8,128)} %bitcast.11, s32[1,64]{1,0:T(1,128)} %bitcast.12, s32[1,128]{1,0:T(1,128)} %bitcast.13), custom_call_target="tpu_custom_call" | custom-call | tf_op jit(solution)/shard_map/pack/pallas_call | solution.py:341
  2.0 23.8 %all_to_all.10.own_ref = bf16[32,120,128]{2,1,0:T(8,128)(2,1)S(1)} all-to-all(bf16[32,120,128]{2,1,0:T(8,128)(2,1)S(1)} %get-tuple-element.16), channel_id=1, replica_groups=mesh['z'=8,'y'=4,'c'=2,'win'=4] {'y','c','win'}, dimensions={0} | all-to-all | bytes 1966080 | tf_op jit(solution)/shard_map/all_to_all | solution.py:363
  25.8 5.7 %collective-permute-start = (bf16[4,120,128]{2,1,0:T(8,128)(2,1)S(1)}, bf16[4,120,128]{2,1,0:T(8,128)(2,1)S(1)}, u32[]{:S(2)}, u32[]{:S(2)}) collective-permute-start(bf16[4,120,128]{2,1,0:T(8,128)(2,1)S(1)} %slice.8), channel_id=1, source_target_pairs={{32,0},{64,32},{96,64},{128,96},{160,128},{192,160},{224,192},{0,2... | collective-permute-start | bytes 368648 | tf_op jit(solution)/shard_map/ppermute | solution.py:366
  31.5 0.1 collective-permute-start.1
  31.6 5.7 %cross.1 = (f32[128,128]{1,0:T(8,128)S(1)}, bf16[128,512]{1,0:T(8,128)(2,1)S(1)}, f32[7,136,128]{2,1,0:T(8,128)S(1)}, f32[7,136,128]{2,1,0:T(8,128)S(1)}, f32[7,...) custom-call(bf16[32,120,128]{2,1,0:T(8,128)(2,1)S(1)} %all_to_all.10, ...), custom_call_target="tpu_custom_call" | custom-call | tf_op jit(solution)/shard_map/cross/pallas_call | solution.py:369
  37.3 0.0 collective-permute-done.1.before_ref
  37.3 0.0 collective-permute-done.after_ref
  37.3 1.3 %edge.1 = f32[256,128]{1,0:T(8,128)S(1)} custom-call(bf16[4,120,128]{2,1,0:T(8,128)(2,1)S(1)} %collective-permute-done.after_ref, bf16[4,112,128]{2,1,0:T(8,128)(2,1)S(1)} %collective-permute-done.1.before_ref, f32[128,128]{1,0:T(8,128)S(1)} %get-tuple-element.19.part_ref, bf16[128,512]{1,0:T(8,128)(2,1)S(1)} %get-tuple-element.20.hot_ref, ...), custom_call_target="tpu_custom_call" | custom-call | tf_op jit(solution)/shard_map/edge/pallas_call | solution.py:392
  38.6 21.2 %all_to_all.11 = f32[256,1,128]{2,1,0:T(1,128)S(1)} all-to-all(f32[256,1,128]{2,1,0:T(1,128)S(1)} %bitcast.8), channel_id=1, replica_groups=mesh['z'=8,'y'=4,'c'=2,'win'=4] {'z','y','c','win'}, dimensions={0} | all-to-all | bytes 262144 | tf_op jit(solution)/shard_map/all_to_all | solution.py:408
  59.8 0.7 %finish.1 = f32[4,1024]{1,0:T(4,128)} custom-call(f32[8,32,128]{2,1,0:T(8,128)S(1)} %bitcast.9), custom_call_target="tpu_custom_call" | custom-call | tf_op jit(solution)/shard_map/finish/pallas_call | solution.py:410
  (2 shorter events, 0.0 us)
Async XLA Ops:
  25.8 11.5 %collective-permute-start = (bf16[4,120,128]{2,1,0:T(8,128)(2,1)S(1)}, bf16[4,120,128]{2,1,0:T(8,128)(2,1)S(1)}, u32[]{:S(2)}, u32[]{:S(2)}) collective-permute-start(bf16[4,120,128]{2,1,0:T(8,128)(2,1)S(1)} %slice.8), channel_id=1, source_target_pairs={{32,0},{64,32},{96,64},{128,96},{160,128},{192,160},{224,192},{0,2... | collective-permute-start | bytes 368648 | tf_op jit(solution)/shard_map/ppermute | solution.py:366
  31.5 5.8 %collective-permute-start.1 = (bf16[4,112,128]{2,1,0:T(8,128)(2,1)S(1)}, bf16[4,112,128]{2,1,0:T(8,128)(2,1)S(1)}, u32[]{:S(2)}, u32[]{:S(2)}) collective-permute-start(bf16[4,112,128]{2,1,0:T(8,128)(2,1)S(1)} %slice.9), channel_id=1, source_target_pairs={{0,32},{32,64},{64,96},{96,128},{128,160},{160,192},{192,224},{224... | collective-permute-start | bytes 344072 | tf_op jit(solution)/shard_map/ppermute | solution.py:365

commit v8 on v7

--- a/solution.py
+++ b/solution.py
@@ -288,10 +288,7 @@
             bins_ref[...] == wanted, jnp.ones((LANES, LANES), BF16), jnp.zeros((LANES, LANES), BF16))
 
     x_ref[3 * LANES + 64:4 * LANES, :] = jnp.zeros((64, LANES), BF16)
-    for unit in range(STA + 4):
-        here = unit < STA
-        own_t, own_s, place = (t_ref, s_ref, unit) if here else (after_t_ref, after_s_ref, unit - STA)
-        other_m, other_d = (m_ref, d_ref) if here else (own_m_ref, own_d_ref)
+    def products(own_t, own_s, place, other_m, other_d, base):
         k1, k23 = {}, {}
         for w in range(WIN):
             rows = pl.ds(w, 8, stride=PITCH)
@@ -303,11 +300,19 @@
             for n in range(4):
                 v = total * other_d[n, rows, :]
                 k1[n] = v if w == 0 else k1[n] + v
-        base = (unit if here else unit + 1) * 64
         for n in range(4):
             lower, upper = spread_of(k1[n])
             values = [lower - k23[2 * n], upper - k23[2 * n + 1] if n < 3 else zero]
-            x_ref[base + n * 16:base + (n + 1) * 16, :] = jnp.concatenate(values, axis=0).astype(BF16)
+            x_ref[pl.ds(base + n * 16, 16), :] = jnp.concatenate(values, axis=0).astype(BF16)
+
+    def unit_pair(n, carry):
+        products(t_ref, s_ref, n, m_ref, d_ref, pl.multiple_of(n * 64, 64))
+        products(after_t_ref, after_s_ref, n, own_m_ref, own_d_ref, pl.multiple_of(4 * LANES + n * 64, 64))
+        return carry
+
+    lax.fori_loop(0, 4, unit_pair, 0)
+    for unit in range(4, STA):
+        products(t_ref, s_ref, unit, m_ref, d_ref, unit * 64)
     total = part_ref[...] + jnp.dot(hot_ref[...], x_ref[0:4 * LANES, :], preferred_element_type=F32)
     total = total + jnp.dot(after_hot_ref[...], x_ref[4 * LANES:, :], preferred_element_type=F32)
     parts = []

time: 60.7 us -> 60.7 us (level)
  no operation moved by 1% of the time
where the time goes in v8:
time: 60.7 us; the launch traced here: 60.6 us
  blocking collectives  45 us (74%)
  Pallas kernels  9.73 us (16%)
  starting transfers between devices  5.74 us (9%)
    all_to_all x1, blocking collectives, on_device(): own = lax.all_to_all(packed, ('y', 'c', 'win'), 0, 0)  23.8 us
    all_to_all x1, blocking collectives, on_device(): lax.all_to_all(send.reshape(256, 1, LANES), ('z', 'y', 'c', 'win'), 0, 0)  21.2 us
    pallas_call x1, Pallas kernels, on_device(): pl.pallas_call(cross_kernel, out_shape=(pltpu.VMEM((LANES, LANES), F32),...  5.71 us
    ppermute x1, starting transfers between devices, on_device(): lax.ppermute(own[0:4], 'z', [((i + 1) % count, i) for i in range(count)])  5.65 us
    pallas_call x1, Pallas kernels, on_device(): pl.pallas_call(pack_kernel, out_shape=(pltpu.VMEM((32, MSG, LANES), BF16)...  1.95 us
    pallas_call x1, Pallas kernels, on_device(): pl.pallas_call(edge_kernel, out_shape=pltpu.VMEM((256, LANES), F32), in_s...  1.36 us
  transfers between devices with their start and end apart: 2, of which 0 were waited for; matrix products, arithmetic and copies ran while one was open for 0% of the time, Pallas kernels for 9%

profile of v8, /device:TPU:1, one launch (start us, length us, event | category | flops | bytes accessed | tf_op | source)
XLA Modules:
  0.0 60.6 jit_solution(10795859754680095965)
XLA Ops:
  0.0 2.0 %pack.1 = (bf16[32,120,128]{2,1,0:T(8,128)(2,1)S(1)}, s32[1,64]{1,0:T(1,128)S(1)}, s32[1,128]{1,0:T(1,128)S(1)}) custom-call(bf16[7,16,4096]{2,1,0:T(8,128)(2,1)} %bitcast.10, s32[3,7,7]{2,1,0:T(8,128)} %bitcast.11, s32[1,64]{1,0:T(1,128)} %bitcast.12, s32[1,128]{1,0:T(1,128)} %bitcast.13), custom_call_target="tpu_custom_call" | custom-call | tf_op jit(solution)/shard_map/pack/pallas_call | solution.py:346
  2.0 23.8 %all_to_all.10.own_ref = bf16[32,120,128]{2,1,0:T(8,128)(2,1)S(1)} all-to-all(bf16[32,120,128]{2,1,0:T(8,128)(2,1)S(1)} %get-tuple-element.16), channel_id=1, replica_groups=mesh['z'=8,'y'=4,'c'=2,'win'=4] {'y','c','win'}, dimensions={0} | all-to-all | bytes 1966080 | tf_op jit(solution)/shard_map/all_to_all | solution.py:368
  25.8 5.7 %collective-permute-start = (bf16[4,120,128]{2,1,0:T(8,128)(2,1)S(1)}, bf16[4,120,128]{2,1,0:T(8,128)(2,1)S(1)}, u32[]{:S(2)}, u32[]{:S(2)}) collective-permute-start(bf16[4,120,128]{2,1,0:T(8,128)(2,1)S(1)} %slice.8), channel_id=1, source_target_pairs={{32,0},{64,32},{96,64},{128,96},{160,128},{192,160},{224,192},{0,2... | collective-permute-start | bytes 368648 | tf_op jit(solution)/shard_map/ppermute | solution.py:371
  31.5 0.1 collective-permute-start.1
  31.6 5.7 %cross.1 = (f32[128,128]{1,0:T(8,128)S(1)}, bf16[128,512]{1,0:T(8,128)(2,1)S(1)}, f32[7,136,128]{2,1,0:T(8,128)S(1)}, f32[7,136,128]{2,1,0:T(8,128)S(1)}, f32[7,...) custom-call(bf16[32,120,128]{2,1,0:T(8,128)(2,1)S(1)} %all_to_all.10, ...), custom_call_target="tpu_custom_call" | custom-call | tf_op jit(solution)/shard_map/cross/pallas_call | solution.py:374
  37.3 0.0 collective-permute-done.1.before_ref
  37.3 0.0 collective-permute-done.after_ref
  37.3 1.4 %edge.1 = f32[256,128]{1,0:T(8,128)S(1)} custom-call(bf16[4,120,128]{2,1,0:T(8,128)(2,1)S(1)} %collective-permute-done.after_ref, bf16[4,112,128]{2,1,0:T(8,128)(2,1)S(1)} %collective-permute-done.1.before_ref, f32[128,128]{1,0:T(8,128)S(1)} %get-tuple-element.19.part_ref, bf16[128,512]{1,0:T(8,128)(2,1)S(1)} %get-tuple-element.20.hot_ref, ...), custom_call_target="tpu_custom_call" | custom-call | tf_op jit(solution)/shard_map/edge/pallas_call | solution.py:397
  38.7 21.2 %all_to_all.11 = f32[256,1,128]{2,1,0:T(1,128)S(1)} all-to-all(f32[256,1,128]{2,1,0:T(1,128)S(1)} %bitcast.8), channel_id=1, replica_groups=mesh['z'=8,'y'=4,'c'=2,'win'=4] {'z','y','c','win'}, dimensions={0} | all-to-all | bytes 262144 | tf_op jit(solution)/shard_map/all_to_all | solution.py:413
  59.9 0.7 %finish.1 = f32[4,1024]{1,0:T(4,128)} custom-call(f32[8,32,128]{2,1,0:T(8,128)S(1)} %bitcast.9), custom_call_target="tpu_custom_call" | custom-call | tf_op jit(solution)/shard_map/finish/pallas_call | solution.py:415
  (2 shorter events, 0.0 us)
Async XLA Ops:
  25.8 11.5 %collective-permute-start = (bf16[4,120,128]{2,1,0:T(8,128)(2,1)S(1)}, bf16[4,120,128]{2,1,0:T(8,128)(2,1)S(1)}, u32[]{:S(2)}, u32[]{:S(2)}) collective-permute-start(bf16[4,120,128]{2,1,0:T(8,128)(2,1)S(1)} %slice.8), channel_id=1, source_target_pairs={{32,0},{64,32},{96,64},{128,96},{160,128},{192,160},{224,192},{0,2... | collective-permute-start | bytes 368648 | tf_op jit(solution)/shard_map/ppermute | solution.py:371
  31.5 5.8 %collective-permute-start.1 = (bf16[4,112,128]{2,1,0:T(8,128)(2,1)S(1)}, bf16[4,112,128]{2,1,0:T(8,128)(2,1)S(1)}, u32[]{:S(2)}, u32[]{:S(2)}) collective-permute-start(bf16[4,112,128]{2,1,0:T(8,128)(2,1)S(1)} %slice.9), channel_id=1, source_target_pairs={{0,32},{32,64},{64,96},{96,128},{128,160},{160,192},{192,224},{224... | collective-permute-start | bytes 344072 | tf_op jit(solution)/shard_map/ppermute | solution.py:370

commit v9 on v7

--- a/solution.py
+++ b/solution.py
@@ -59,8 +59,8 @@
     row8 = lax.broadcasted_iota(jnp.int32, (STA, LANES), 0)
     labels = jnp.zeros((STA, LANES), F32)
     for r in range(ROUNDS):
-        place = jnp.where(lane8 == row8 + 8 * r, 1.0, 0.0).astype(F32)
-        labels = labels + jnp.dot(bins_ref[r].astype(F32), place, preferred_element_type=F32)
+        place = jnp.where(lane8 == row8 + 8 * r, 1.0, 0.0).astype(BF16)
+        labels = labels + jnp.dot(bins_ref[r].astype(F32).astype(BF16), place, preferred_element_type=F32)
     labels = jnp.concatenate([labels, jnp.zeros((1, LANES), F32)], axis=0).astype(BF16)
     for d in range(32):
         out_ref[d, ROWS:MSG, :] = labels

time: 60.7 us -> 60.7 us (level)
  no operation moved by 1% of the time
where the time goes in v9:
time: 60.7 us; the launch traced here: 60.5 us
  blocking collectives  45 us (74%)
  Pallas kernels  9.71 us (16%)
  starting transfers between devices  5.74 us (9%)
    all_to_all x1, blocking collectives, on_device(): own = lax.all_to_all(packed, ('y', 'c', 'win'), 0, 0)  23.8 us
    all_to_all x1, blocking collectives, on_device(): lax.all_to_all(send.reshape(256, 1, LANES), ('z', 'y', 'c', 'win'), 0, 0)  21.2 us
    pallas_call x1, Pallas kernels, on_device(): pl.pallas_call(cross_kernel, out_shape=(pltpu.VMEM((LANES, LANES), F32),...  5.7 us
    ppermute x1, starting transfers between devices, on_device(): lax.ppermute(own[0:4], 'z', [((i + 1) % count, i) for i in range(count)])  5.65 us
    pallas_call x1, Pallas kernels, on_device(): pl.pallas_call(pack_kernel, out_shape=(pltpu.VMEM((32, MSG, LANES), BF16)...  1.96 us
    pallas_call x1, Pallas kernels, on_device(): pl.pallas_call(edge_kernel, out_shape=pltpu.VMEM((256, LANES), F32), in_s...  1.34 us
  transfers between devices with their start and end apart: 2, of which 0 were waited for; matrix products, arithmetic and copies ran while one was open for 0% of the time, Pallas kernels for 9%

profile of v9, /device:TPU:1, one launch (start us, length us, event | category | flops | bytes accessed | tf_op | source)
XLA Modules:
  0.0 60.5 jit_solution(14286677820811347018)
XLA Ops:
  0.0 2.0 %pack.1 = (bf16[32,120,128]{2,1,0:T(8,128)(2,1)S(1)}, s32[1,64]{1,0:T(1,128)S(1)}, s32[1,128]{1,0:T(1,128)S(1)}) custom-call(bf16[7,16,4096]{2,1,0:T(8,128)(2,1)} %bitcast.10, s32[3,7,7]{2,1,0:T(8,128)} %bitcast.11, s32[1,64]{1,0:T(1,128)} %bitcast.12, s32[1,128]{1,0:T(1,128)} %bitcast.13), custom_call_target="tpu_custom_call" | custom-call | tf_op jit(solution)/shard_map/pack/pallas_call | solution.py:341
  2.0 23.8 %all_to_all.10.own_ref = bf16[32,120,128]{2,1,0:T(8,128)(2,1)S(1)} all-to-all(bf16[32,120,128]{2,1,0:T(8,128)(2,1)S(1)} %get-tuple-element.16), channel_id=1, replica_groups=mesh['z'=8,'y'=4,'c'=2,'win'=4] {'y','c','win'}, dimensions={0} | all-to-all | bytes 1966080 | tf_op jit(solution)/shard_map/all_to_all | solution.py:363
  25.8 5.7 %collective-permute-start = (bf16[4,120,128]{2,1,0:T(8,128)(2,1)S(1)}, bf16[4,120,128]{2,1,0:T(8,128)(2,1)S(1)}, u32[]{:S(2)}, u32[]{:S(2)}) collective-permute-start(bf16[4,120,128]{2,1,0:T(8,128)(2,1)S(1)} %slice.8), channel_id=1, source_target_pairs={{32,0},{64,32},{96,64},{128,96},{160,128},{192,160},{224,192},{0,2... | collective-permute-start | bytes 368648 | tf_op jit(solution)/shard_map/ppermute | solution.py:366
  31.5 0.1 collective-permute-start.1
  31.6 5.7 %cross.1 = (f32[128,128]{1,0:T(8,128)S(1)}, bf16[128,512]{1,0:T(8,128)(2,1)S(1)}, f32[7,136,128]{2,1,0:T(8,128)S(1)}, f32[7,136,128]{2,1,0:T(8,128)S(1)}, f32[7,...) custom-call(bf16[32,120,128]{2,1,0:T(8,128)(2,1)S(1)} %all_to_all.10, ...), custom_call_target="tpu_custom_call" | custom-call | tf_op jit(solution)/shard_map/cross/pallas_call | solution.py:369
  37.3 0.0 collective-permute-done.1.before_ref
  37.3 0.0 collective-permute-done.after_ref
  37.3 1.3 %edge.1 = f32[256,128]{1,0:T(8,128)S(1)} custom-call(bf16[4,120,128]{2,1,0:T(8,128)(2,1)S(1)} %collective-permute-done.after_ref, bf16[4,112,128]{2,1,0:T(8,128)(2,1)S(1)} %collective-permute-done.1.before_ref, f32[128,128]{1,0:T(8,128)S(1)} %get-tuple-element.19.part_ref, bf16[128,512]{1,0:T(8,128)(2,1)S(1)} %get-tuple-element.20.hot_ref, ...), custom_call_target="tpu_custom_call" | custom-call | tf_op jit(solution)/shard_map/edge/pallas_call | solution.py:392
  38.6 21.2 %all_to_all.11 = f32[256,1,128]{2,1,0:T(1,128)S(1)} all-to-all(f32[256,1,128]{2,1,0:T(1,128)S(1)} %bitcast.8), channel_id=1, replica_groups=mesh['z'=8,'y'=4,'c'=2,'win'=4] {'z','y','c','win'}, dimensions={0} | all-to-all | bytes 262144 | tf_op jit(solution)/shard_map/all_to_all | solution.py:408
  59.8 0.7 %finish.1 = f32[4,1024]{1,0:T(4,128)} custom-call(f32[8,32,128]{2,1,0:T(8,128)S(1)} %bitcast.9), custom_call_target="tpu_custom_call" | custom-call | tf_op jit(solution)/shard_map/finish/pallas_call | solution.py:410
  (2 shorter events, 0.0 us)
Async XLA Ops:
  25.8 11.5 %collective-permute-start = (bf16[4,120,128]{2,1,0:T(8,128)(2,1)S(1)}, bf16[4,120,128]{2,1,0:T(8,128)(2,1)S(1)}, u32[]{:S(2)}, u32[]{:S(2)}) collective-permute-start(bf16[4,120,128]{2,1,0:T(8,128)(2,1)S(1)} %slice.8), channel_id=1, source_target_pairs={{32,0},{64,32},{96,64},{128,96},{160,128},{192,160},{224,192},{0,2... | collective-permute-start | bytes 368648 | tf_op jit(solution)/shard_map/ppermute | solution.py:366
  31.5 5.8 %collective-permute-start.1 = (bf16[4,112,128]{2,1,0:T(8,128)(2,1)S(1)}, bf16[4,112,128]{2,1,0:T(8,128)(2,1)S(1)}, u32[]{:S(2)}, u32[]{:S(2)}) collective-permute-start(bf16[4,112,128]{2,1,0:T(8,128)(2,1)S(1)} %slice.9), channel_id=1, source_target_pairs={{0,32},{32,64},{64,96},{96,128},{128,160},{160,192},{192,224},{224... | collective-permute-start | bytes 344072 | tf_op jit(solution)/shard_map/ppermute | solution.py:365
